TPU v7x, 768 devices: a whole 4x8x12 slice. The times are simulated.
768 devices in a mesh: sx: 64 (over y, x, core), sy: 12 (over z).
Axes of the slice: x: 4, y: 8, z: 12, core: 2. Of those that a mesh axis runs over, the one named last changes fastest.
Arguments:
- background: bfloat16 [1536, 768, 762], P('sx', 'sy'), may hold values from -6 to 6
- slab_owner: int32 [762], replicated, may hold values from 0 to 767, as said below
- class_length_scale: float32 [16], replicated, may hold values from 0.5 to 16
- band_widths: int32 [16], replicated, may hold values from 1 to 32, as said below
- x_class: int32 [6, 1536], replicated, may hold values from 0 to 15
- y_class: int32 [6, 768], replicated, may hold values from 0 to 15
- z_class: int32 [6, 127], replicated, may hold values from 0 to 15
Outputs:
- filtered_row_energy: float32 [768, 1536], P(('sx', 'sy'))
- covariance_applied: bfloat16 [1536, 768, 762], P('sx', 'sy')
Inputs may be any that keep to these rules, and one draw needn't show every extreme that they name: `slab_owner`: each device owns at most 1 slabs, and some device owns exactly 1. `band_widths`: some class has band half-width exactly 32.
All inputs are finite; a program needn't handle non-finite values.
Results may differ from a plain program's by a relative error of at most 0.0076.
Values may be sent and summed in bfloat16 or wider, within the bound.
A program may use at most 64 MiB of HBM per device.

v0:
```python
import jax
import jax.numpy as jnp
from jax import lax
from jax.sharding import PartitionSpec as P

K = 1


def profile(row_index, col_index, row_class, class_length_scale, band_widths, limit):
    onehot = row_class[..., None] == jnp.arange(class_length_scale.shape[0], dtype=jnp.int32)
    scale = jnp.sum(jnp.where(onehot, class_length_scale, jnp.float32(0.0)), -1)
    reach = jnp.sum(jnp.where(onehot, band_widths, 0), -1)
    offset = col_index - row_index
    inside = (jnp.abs(offset) <= reach) & (col_index >= 0) & (col_index < limit)
    ratio = offset.astype(jnp.float32) / scale
    return jnp.where(inside, jnp.exp(-0.5 * ratio * ratio), jnp.float32(0.0))


def dense_weights(classes, class_length_scale, band_widths):
    count = classes.shape[0]
    index = jnp.arange(count, dtype=jnp.int32)
    bump = profile(
        index[:, None], index[None, :], classes[:, None], class_length_scale, band_widths, count
    )
    return (bump * lax.rsqrt(jnp.sum(bump * bump, -1, keepdims=True))).astype(jnp.bfloat16)


def block_weights(classes, class_length_scale, band_widths, block):
    count = classes.shape[0]
    nblock = count // block
    row_index = (
        jnp.arange(nblock, dtype=jnp.int32)[:, None] * block
        + jnp.arange(block, dtype=jnp.int32)[None, :]
    )
    shifts = jnp.arange(-1, 2, dtype=jnp.int32)
    col_index = (
        jnp.arange(nblock, dtype=jnp.int32)[None, :, None, None] + shifts[:, None, None, None]
    ) * block + jnp.arange(block, dtype=jnp.int32)[None, None, None, :]
    row_class = classes.reshape(nblock, block)[None, :, :, None]
    bump = profile(
        row_index[None, :, :, None], col_index, row_class, class_length_scale, band_widths, count
    )
    norm_sq = jnp.sum(bump * bump, axis=(0, 3), keepdims=True)
    return (bump * lax.rsqrt(norm_sq)).astype(jnp.bfloat16)


def gather_pieces(pieces):
    return lax.all_to_all(
        lax.all_to_all(pieces, "sx", split_axis=0, concat_axis=0, tiled=True),
        "sy",
        split_axis=1,
        concat_axis=1,
        tiled=True,
    )


def filter_x(slab, classes, class_length_scale, band_widths, block):
    cells_x, cells_y = slab.shape
    nblock = cells_x // block
    weights = block_weights(classes, class_length_scale, band_widths, block)
    padded = jnp.pad(slab, ((block, block), (0, 0))).reshape(nblock + 2, block, cells_y)
    windows = jnp.stack([padded[start : start + nblock] for start in range(3)])
    result = jnp.einsum("obcy,obrc->bry", windows, weights, preferred_element_type=jnp.float32)
    return result.reshape(cells_x, cells_y).astype(jnp.bfloat16)


def filter_y(x_filtered, classes, class_length_scale, band_widths, block):
    cells_x, cells_y = x_filtered.shape
    nblock = cells_y // block
    weights = block_weights(classes, class_length_scale, band_widths, block)
    padded = jnp.pad(x_filtered, ((0, 0), (block, block))).reshape(cells_x, nblock + 2, block)
    windows = jnp.stack([padded[:, start : start + nblock, :] for start in range(3)])
    result = jnp.einsum("oxbc,obrc->xbr", windows, weights, preferred_element_type=jnp.float32)
    return result.reshape(cells_x, cells_y)


def per_device(background, slab_owner, class_length_scale, band_widths, x_class, y_class, z_class):
    local_x, local_y, nslab = background.shape
    nvars, levels = z_class.shape
    count_sx = lax.axis_size("sx")
    count_sy = lax.axis_size("sy")
    cells_x = local_x * count_sx
    cells_y = local_y * count_sy
    order = jnp.arange(nslab, dtype=jnp.int32)
    same = (slab_owner[:, None] == slab_owner[None, :]) & (order[None, :] < order[:, None])
    rank = jnp.sum(same.astype(jnp.int32), 1)
    position = slab_owner * K + rank
    table = jnp.full((count_sx * count_sy * K,), nslab, jnp.int32).at[position].set(order)
    flat = background.reshape(local_x * local_y, nslab).T
    extended = jnp.concatenate([flat, jnp.zeros((1, local_x * local_y), jnp.bfloat16)], 0)
    outgoing = jnp.take(extended, table, axis=0).reshape(count_sx, count_sy, K, local_x * local_y)
    arrived = gather_pieces(outgoing)
    slabs = (
        arrived.reshape(count_sx, count_sy, K, local_x, local_y)
        .transpose(2, 0, 3, 1, 4)
        .reshape(K, cells_x, cells_y)
    )
    myself = lax.axis_index("sx") * count_sy + lax.axis_index("sy")
    held = lax.dynamic_slice_in_dim(table, myself * K, K)
    control_variable = jnp.minimum(held, nslab - 1) // levels
    x_filtered = filter_x(
        slabs[0], x_class[control_variable[0]], class_length_scale, band_widths, local_y
    )
    results = [
        filter_y(x_filtered, y_class[control_variable[0]], class_length_scale, band_widths, local_y)
    ]
    y_slab = jnp.stack(results)
    filtered_row_energy = jnp.sum(y_slab * y_slab, 2)
    outbound = y_slab.astype(jnp.bfloat16).reshape(K, count_sx, local_x, count_sy, local_y)
    outbound = outbound.transpose(1, 3, 0, 2, 4).reshape(count_sx, count_sy, K, local_x * local_y)
    output_field = gather_pieces(outbound).reshape(count_sx * count_sy * K, local_x * local_y)
    column_blocks = jnp.take(output_field, position, axis=0).reshape(
        nvars, levels, local_x * local_y
    )
    vertical_weight = jax.vmap(lambda c: dense_weights(c, class_length_scale, band_widths))(z_class)
    covariance_result = jnp.einsum(
        "poh,phw->pow", vertical_weight, column_blocks, preferred_element_type=jnp.float32
    )
    covariance_result = covariance_result.astype(jnp.bfloat16).reshape(nslab, local_x * local_y).T
    return (filtered_row_energy, covariance_result.reshape(local_x, local_y, nslab))


def solution(mesh):
    in_specs = (P("sx", "sy", None), P(), P(), P(), P(), P(), P())
    out_specs = (P(("sx", "sy"), None), P("sx", "sy", None))
    return jax.shard_map(
        per_device, mesh=mesh, in_specs=in_specs, out_specs=out_specs, check_vma=False
    )
```

profile of v0, /device:TPU:1, one launch (start us, length us, event | category | flops | bytes accessed | tf_op | source)
XLA Modules:
  0.0 445.8 jit_solution(6296062381867403566)
XLA Ops:
  0.6 1.1 convert_reduce_fusion
  1.8 0.7 compare_and_fusion
  2.5 4.1 scatter_custom_fusion
  6.6 0.1 broadcast_in_dim.134
  6.7 4.3 copy.39
  11.0 1.8 concatenate.3
  12.8 3.8 gather_fusion
  16.6 3.4 gather.13
  20.0 0.4 select_bitcast_fusion
  20.4 86.7 %all_to_all.20 = bf16[64,12,1,1536]{3,1,2,0:T(8,128)(2,1)S(1)} all-to-all(bf16[64,12,1,1536]{3,1,2,0:T(8,128)(2,1)S(1)} %select_bitcast_fusion), channel_id=1, replica_groups=mesh['sx'=64,'sy'=12] {'sx'}, dimensions={0} | all-to-all | bytes 4718592 | tf_op jit(solution)/shard_map/all_to_all | solution.py:49
  107.1 2.7 copy.41
  109.8 12.6 %all-to-all-start.1 = ((bf16[64,12,1,1536]{3,0,2,1:T(8,128)(2,1)}), bf16[64,12,1,1536]{3,0,2,1:T(8,128)(2,1)S(1)}, u32[]{:S(2)}, u32[]{:S(2)}) async-start(bf16[64,12,1,1536]{3,0,2,1:T(8,128)(2,1)} %copy.41), calls=%async_computation.1 | async-start | bytes 4718592 | tf_op jit(solution)/shard_map/all_to_all | solution.py:48
  122.4 0.6 dynamic_slice.9
  123.7 0.8 dynamic-slice_reduce_fusion.1
  125.1 1.1 multiply_reduce_fusion.1
  126.2 0.1 select_reduce_fusion
  126.3 0.1 select_reduce_fusion.1
  126.5 0.1 fusion.49
  126.7 2.0 multiply_reduce_fusion
  128.7 70.4 %all-to-all-done.1 = bf16[64,12,1,1536]{3,0,2,1:T(8,128)(2,1)S(1)} async-done(((bf16[64,12,1,1536]{3,0,2,1:T(8,128)(2,1)}), bf16[64,12,1,1536]{3,0,2,1:T(8,128)(2,1)S(1)}, u32[]{:S(2)}, u32[]{:S(2)}) %all-to-all-start.1) | async-done | bytes 2359328 | tf_op jit(solution)/shard_map/all_to_all | solution.py:48
  199.1 4.6 %reshape.338 = bf16[64,12,1,24,64]{4,3,0,1,2:T(8,128)(2,1)} reshape(bf16[64,12,1,1536]{3,0,2,1:T(8,128)(2,1)S(1)} %all-to-all-done.1) | data formatting | bytes 4718592 | tf_op jit(solution)/shard_map/reshape | solution.py:94
  203.7 10.7 %copy.42 = bf16[1,64,24,12,64]{4,3,2,1,0:T(8,128)(2,1)} copy(bf16[1,64,24,12,64]{4,2,1,3,0:T(8,128)(2,1)} %bitcast.52) | data formatting | bytes 4718592 | tf_op jit(solution)/shard_map/transpose | solution.py:95
  214.3 8.4 %stack.25 = bf16[1,24,64,768]{3,2,1,0:T(8,128)(2,1)} reshape(bf16[1,64,24,12,64]{4,3,2,1,0:T(8,128)(2,1)} %copy.42) | data formatting | bytes 4718592 | tf_op jit(solution)/shard_map/stack | solution.py:62
  222.7 7.2 %squeeze_reshape.3 = bf16[1536,768]{1,0:T(8,128)(2,1)S(1)} reshape(bf16[1,64,24,12,64]{4,3,2,1,0:T(8,128)(2,1)} %copy.42) | data formatting | bytes 4718592 | tf_op jit(solution)/shard_map/squeeze;reshape | solution.py:102
  230.0 0.3 pad_slice_fusion.1
  230.3 1.3 copy-done.2
  231.6 4.7 %bitcast_convert_fusion.1 = bf16[24,64,768]{2,1,0:T(8,128)(2,1)} fusion(bf16[1,24,64,768]{3,2,0,1:T(8,128)(2,1)S(1)} %bitcast.56, bf16[1,24,64,768]{3,2,0,1:T(8,128)(2,1)S(1)} %bitcast.60, bf16[1,24,64,768]{3,2,0,1:T(8,128)(2,1)S(1)} %bitcast.55, f32[24,64]{1,0:T(8,128)S(1)} %rsqrt.25, f32[24,64]{1,0:T(8,128)S(1)} %select_reduce_fusion, ...), kind=kOutput, calls=%fused_computation.18 | convolution fusion | flops 464781312 | bytes 9489408 | tf_op jit(solution)/shard_map/obcy,obrc->bry/dot_general | solution.py:63
  236.3 2.8 copy.55
  239.1 0.2 pad.10.clone
  239.3 0.8 slice_bitcast_fusion.2
  240.2 2.9 fusion.12
  243.1 0.2 fusion.17
  243.2 3.9 copy.48
  247.2 6.2 %reshape.340 = bf16[64,12,1,1536]{3,0,1,2:T(8,128)(2,1)S(1)} reshape(bf16[64,12,1,24,64]{4,3,0,1,2:T(8,128)(2,1)} %bitcast.51) | data formatting | bytes 4718592 | tf_op jit(solution)/shard_map/reshape | solution.py:110
  253.3 1.3 copy.49
  254.7 87.1 %all_to_all.21 = bf16[64,12,1,1536]{3,1,2,0:T(8,128)(2,1)S(1)} all-to-all(bf16[64,12,1,1536]{3,1,2,0:T(8,128)(2,1)S(1)} %copy.49), channel_id=1, replica_groups=mesh['sx'=64,'sy'=12] {'sx'}, dimensions={0} | all-to-all | bytes 4718592 | tf_op jit(solution)/shard_map/all_to_all | solution.py:49
  341.8 2.7 copy.50
  344.5 3.9 all-to-all-start.3
  348.7 0.4 multiply_reduce_fusion.2
  349.1 0.6 reduce_sum.109
  349.7 76.4 %all-to-all-done.3 = bf16[64,12,1,1536]{3,0,2,1:T(8,128)(2,1)S(1)} async-done(((bf16[64,12,1,1536]{3,0,2,1:T(8,128)(2,1)}), bf16[64,12,1,1536]{3,0,2,1:T(8,128)(2,1)S(1)}, u32[]{:S(2)}, u32[]{:S(2)}) %all-to-all-start.3) | async-done | bytes 2359328 | tf_op jit(solution)/shard_map/all_to_all | solution.py:48
  426.1 3.0 copy.51
  429.1 3.6 reshape.341
  432.7 3.8 gather_fusion.1
  436.5 2.3 gather.15
  438.8 2.2 convolution_convert_fusion
  441.0 2.3 reshape.342
  443.4 2.4 copy.52
  (39 shorter events, 1.1 us)
Async XLA Ops:
  0.6 123.9 %copy-start = (s32[6,1536]{1,0:T(8,128)S(1)}, s32[6,1536]{1,0:T(8,128)}, u32[]{:S(2)}) copy-start(s32[6,1536]{1,0:T(8,128)} %param.11) | copy-start | bytes 110596
  109.8 14.8 %copy-start.4 = (f32[16]{0:T(128)S(1)}, f32[16]{0:T(128)}, u32[]{:S(2)}) copy-start(f32[16]{0:T(128)} %param.9) | copy-start | bytes 196
  109.8 14.9 %copy-start.5 = (s32[16]{0:T(128)S(1)}, s32[16]{0:T(128)}, u32[]{:S(2)}) copy-start(s32[16]{0:T(128)} %param.10) | copy-start | bytes 196
  109.8 89.3 %all-to-all-start.1 = ((bf16[64,12,1,1536]{3,0,2,1:T(8,128)(2,1)}), bf16[64,12,1,1536]{3,0,2,1:T(8,128)(2,1)S(1)}, u32[]{:S(2)}, u32[]{:S(2)}) async-start(bf16[64,12,1,1536]{3,0,2,1:T(8,128)(2,1)} %copy.41), calls=%async_computation.1 | async-start | bytes 4718592 | tf_op jit(solution)/shard_map/all_to_all | solution.py:48
  229.9 1.7 copy-start.2
  344.5 4.0 copy-start.3
  344.5 81.6 %all-to-all-start.3 = ((bf16[64,12,1,1536]{3,0,2,1:T(8,128)(2,1)}), bf16[64,12,1,1536]{3,0,2,1:T(8,128)(2,1)S(1)}, u32[]{:S(2)}, u32[]{:S(2)}) async-start(bf16[64,12,1,1536]{3,0,2,1:T(8,128)(2,1)} %copy.50), calls=%async_computation.3 | async-start | bytes 4718592 | tf_op jit(solution)/shard_map/all_to_all | solution.py:48
  443.4 2.5 copy-start.1
where the time goes:
time: 453 us; the launch traced here: 446 us
  blocking collectives  174 us (38%)
  waiting for transfers between devices  147 us (32%)
  local copies, waits for them, and re-layouts  90.5 us (20%)
  starting transfers between devices  16.4 us (4%)
  matrix products  9.76 us (2%)
  other arithmetic  6.8 us (2%)
    all_to_all x2, blocking collectives, gather_pieces(): lax.all_to_all(pieces, 'sx', split_axis=0, concat_axis=0, tiled=True)  174 us
    all_to_all x2, waiting for transfers between devices, gather_pieces(): lax.all_to_all(lax.all_to_all(pieces, 'sx', split_axis=0, concat_axis=0,...  147 us
    all_to_all x2, starting transfers between devices, gather_pieces(): lax.all_to_all(lax.all_to_all(pieces, 'sx', split_axis=0, concat_axis=0,...  16.4 us
    transpose x1, local copies, waits for them, and re-layouts, per_device(): slabs = arrived.reshape(count_sx, count_sy, K, local_x, local_y).transpos...  10.7 us
  transfers between devices with their start and end apart: 2, of which 2 were waited for; matrix products, arithmetic and copies ran while one was open for 2% of the time, Pallas kernels for 0%

commit v1 on v0

v1 whole, which is shorter than its diff:
```python
import functools

import jax
import jax.numpy as jnp
from jax import lax
from jax.experimental import pallas as pl
from jax.experimental.pallas import tpu as pltpu
from jax.sharding import PartitionSpec as P

MESH = pl.DeviceIdType.MESH
REACH = 32
LANES = 128
PACK = 16
F32 = jnp.float32
BF16 = jnp.bfloat16


def iota(shape, dim):
    return lax.broadcasted_iota(jnp.int32, shape, dim)


def lookup(classes, table):
    out = jnp.zeros(classes.shape, table.dtype)
    for k in range(table.shape[0]):
        out = jnp.where(classes == k, table[k], out)
    return out


def bump_of(offset, inside, scale):
    ratio = offset.astype(F32) / scale
    return jnp.where(inside, jnp.exp(-0.5 * ratio * ratio), jnp.float32(0.0))


def normalised(bump):
    return bump * lax.rsqrt(jnp.sum(bump * bump, 0, keepdims=True))


def dot_nt(a, b):
    return lax.dot_general(a, b, (((1,), (1,)), ((), ())), preferred_element_type=F32)


def dot_nn(a, b):
    return jnp.dot(a, b, preferred_element_type=F32)


def split3(value):
    high = value.astype(BF16)
    rest = value - high.astype(F32)
    middle = rest.astype(BF16)
    low = (rest - middle.astype(F32)).astype(BF16)
    return high, middle, low


def kernel(
    size_x,
    size_y,
    lev,
    background,
    scale_table,
    reach_table,
    x_class,
    y_class,
    z_class,
    energy_out,
    cov_out,
    raw,
    win,
    xfw,
    yr,
    kron,
    wy,
    wz,
    wxt,
    spread,
    tables,
    raw_sem,
    near_send,
    near_recv,
    side_send,
    side_recv,
):
    lx, ly, nslab = background.shape
    nvar = z_class.shape[0]
    far = REACH - lx
    span = lx + 2 * REACH
    p = lax.axis_index("sx")
    q = lax.axis_index("sy")
    core = lax.rem(p, 2)

    def at_x(step):
        return (lax.rem(p + step + size_x, size_x), q)

    def at_y(step):
        return (p, lax.rem(q + step + size_y, size_y))

    load = pltpu.make_async_copy(background, raw, raw_sem)
    load.start()
    barrier = pltpu.get_barrier_semaphore()
    for peer in (at_x(-2), at_x(-1), at_x(1), at_x(2), at_y(-1), at_y(1)):
        pl.semaphore_signal(barrier, inc=1, device_id=peer, device_id_type=MESH)

    outer = at_x(2 * core - 1)
    partner = at_x(1 - 2 * core)
    beyond = at_x(2 - 4 * core)

    def remote(src, dst, send, recv, peer):
        return pltpu.make_async_remote_copy(
            src_ref=src, dst_ref=dst, send_sem=send, recv_sem=recv, device_id=peer, device_id_type=MESH
        )

    def to_outer(v):
        own = win.at[v, pl.ds(REACH, lx)]
        return remote(own, win.at[v, pl.ds(REACH + lx - 2 * lx * core, lx)], near_send.at[v, 0], near_recv.at[v, 0], outer)

    def to_partner(v):
        own = win.at[v, pl.ds(REACH, lx)]
        return remote(own, win.at[v, pl.ds(far + 2 * lx * core, lx)], near_send.at[v, 1], near_recv.at[v, 1], partner)

    def to_beyond(v):
        own = win.at[v, pl.ds(REACH + (lx - far) * (1 - core), far)]
        return remote(own, win.at[v, pl.ds((span - far) * core, far)], near_send.at[v, 2], near_recv.at[v, 2], beyond)

    def forward(v):
        got = win.at[v, pl.ds(far + (lx - far) + REACH * core, far)]
        return remote(got, win.at[v, pl.ds((span - far) * core, far)], near_send.at[v, 3], near_recv.at[v, 3], partner)

    def to_left(v):
        own = xfw.at[v, :, pl.ds(REACH, REACH)]
        return remote(own, xfw.at[v, :, pl.ds(REACH + ly, REACH)], side_send.at[v, 0], side_recv.at[v, 0], at_y(-1))

    def to_right(v):
        own = xfw.at[v, :, pl.ds(ly, REACH)]
        return remote(own, xfw.at[v, :, pl.ds(0, REACH)], side_send.at[v, 1], side_recv.at[v, 1], at_y(1))

    def align(v):
        @pl.loop(0, lx)
        def _(i):
            win[v, REACH + i] = jnp.zeros((ly, LANES), BF16)
            win[v, REACH + i, :, 0:lev] = raw[i, :, lev * v : lev * v + lev]

    load.wait()
    align(0)
    pl.semaphore_wait(barrier, 6)
    for v in range(nvar):
        if v + 1 < nvar:
            align(v + 1)
        to_outer(v).start()
        to_beyond(v).start()
        to_partner(v).start()

    n_x = size_x * lx
    n_y = size_y * ly
    lane_x = iota((n_x, LANES), 1)
    pick_x = ((iota((n_x, LANES), 0) == lx * p + lane_x) & (lane_x < lx)).astype(BF16)
    cls_x = (dot_nn(x_class[...].astype(F32).astype(BF16), pick_x) + 0.5).astype(jnp.int32)
    lane_y = iota((n_y, LANES), 1)
    pick_y = ((iota((n_y, LANES), 0) == ly * q + lane_y) & (lane_y < ly)).astype(BF16)
    cls_y = (dot_nn(y_class[...].astype(F32).astype(BF16), pick_y) + 0.5).astype(jnp.int32)
    scale_x, reach_x = lookup(cls_x, scale_table), lookup(cls_x, reach_table)
    scale_y, reach_y = lookup(cls_y, scale_table), lookup(cls_y, reach_table)
    lane = iota((LANES, LANES), 1)
    depth = iota((LANES, LANES), 0)
    offset = depth - REACH - lane
    col_x = lx * p - REACH + depth
    col_y = ly * q - REACH + depth
    eye = (iota((ly, LANES), 0) == iota((ly, LANES), 1)).astype(BF16)
    for v in range(nvar):
        near = jnp.abs(offset)
        inside = (near <= reach_x[v : v + 1]) & (col_x >= 0) & (col_x < n_x) & (depth < span)
        weight = normalised(bump_of(offset, inside, scale_x[v : v + 1]))
        wxt[v] = jnp.where(lane < lx, weight, 0.0).astype(BF16)
        inside = (near <= reach_y[v : v + 1]) & (col_y >= 0) & (col_y < n_y)
        weight = normalised(bump_of(offset, inside, scale_y[v : v + 1]))
        wy[v] = dot_nt(eye, jnp.where(lane < ly, weight, 0.0).astype(BF16)).astype(BF16)

    spread[...] = (iota(spread.shape, 1) // PACK == iota(spread.shape, 0)).astype(BF16)
    part = lx * PACK // 4

    @pl.loop(0, nvar * 4)
    def _(step):
        v = step // 4
        first = pl.multiple_of((step % 4) * part, 16)
        row = iota((part, LANES), 0) + first
        pick = (row // PACK == iota((part, LANES), 1)).astype(BF16)
        rows = dot_nt(pick, wxt[v]).astype(BF16)
        wide = dot_nn(rows, spread[...])
        same = (iota(wide.shape, 0) % PACK) == (iota(wide.shape, 1) % PACK)
        kron[v, pl.ds(first, part), :] = jnp.where(same, wide, 0.0).astype(BF16)

    tables[...] = jnp.zeros(tables.shape, jnp.int32)
    tables[0:nvar, 0:lev] = z_class[...]
    lane1 = iota((8, LANES), 1)
    for t in range(nvar):
        here = pltpu.roll(tables[...], (LANES - t) % LANES, 1)[t : t + 1]
        if t + 1 < nvar:
            there = pltpu.roll(tables[...], lev - t, 1)[t + 1 : t + 2]
        else:
            there = here
        cls_z = jnp.where(lane1[0:1] < lev - t, here, there)
        scale_z, reach_z = lookup(cls_z, scale_table), lookup(cls_z, reach_table)
        own = lane < lev - t
        offset_z = depth - (lane + t)
        inside = (jnp.abs(offset_z) <= reach_z) & own & (depth < lev)
        upper = normalised(bump_of(offset_z, inside, scale_z))
        wz[t, 0:LANES] = jnp.where(own, upper, 0.0).astype(BF16)
        if t + 1 < nvar:
            offset_z = depth - (lane - (lev - t))
            inside = (jnp.abs(offset_z) <= reach_z) & (lane >= lev - t) & (depth < lev)
            lower = normalised(bump_of(offset_z, inside, scale_z))
            wz[t, LANES : 2 * LANES] = jnp.where(lane >= lev - t, lower, 0.0).astype(BF16)

    def filter_x(v):
        @pl.loop(0, ly // (2 * PACK))
        def _(half):
            first = pl.multiple_of(half * 2 * PACK, 2 * PACK)
            left = win[v, :, pl.ds(first, PACK), :].reshape(span * PACK, LANES)
            right = win[v, :, pl.ds(first + PACK, PACK), :].reshape(span * PACK, LANES)
            got = dot_nn(kron[v], jnp.concatenate([left, right], 1)).astype(BF16)
            got = got.reshape(lx, PACK, 2 * LANES)
            xfw[v, :, pl.ds(first + REACH, PACK), :] = got[:, :, 0:LANES]
            xfw[v, :, pl.ds(first + REACH + PACK, PACK), :] = got[:, :, LANES:]

    def filter_y(v):
        @pl.loop(0, lx // 2)
        def _(pair):
            both = jnp.concatenate([xfw[v, 2 * pair], xfw[v, 2 * pair + 1]], 1)
            got = dot_nn(wy[v], both)
            power = jnp.sum(got * got, 0, keepdims=True)
            for k in range(2):
                piece = got[:, LANES * k : LANES * (k + 1)]
                yr[v, 2 * pair + k] = piece.astype(BF16)
                energy_out[v, pl.ds(2 * pair + k, 1), :] = power[:, LANES * k : LANES * (k + 1)]

    def filter_z(t):
        rows = 4
        width = min(LANES, nslab - LANES * t)

        @pl.loop(0, lx // rows)
        def _(block):
            first = block * rows
            here = yr[t, pl.ds(first, rows)].reshape(rows * ly, LANES)
            if t + 1 < nvar:
                there = yr[t + 1, pl.ds(first, rows)].reshape(rows * ly, LANES)
                got = dot_nn(jnp.concatenate([here, there], 1), wz[t])
            else:
                got = dot_nn(here, wz[t, 0:LANES])
            got = got.astype(BF16).reshape(rows, ly, LANES)
            cov_out[pl.ds(first, rows), :, LANES * t : LANES * t + width] = got[:, :, 0:width]

    for v in range(nvar):
        to_outer(v).wait_recv()
        forward(v).start()
        to_beyond(v).wait_recv()
        to_partner(v).wait_recv()
        if v >= 1:
            to_left(v - 1).wait_recv()
            to_right(v - 1).wait_recv()
            filter_y(v - 1)
        if v >= 2:
            filter_z(v - 2)
        forward(v).wait_recv()
        filter_x(v)
        to_left(v).start()
        to_right(v).start()
    v = nvar - 1
    to_left(v).wait_recv()
    to_right(v).wait_recv()
    filter_y(v)
    filter_z(v - 1)
    filter_z(v)

    for v in range(nvar):
        to_outer(v).wait_send()
        to_beyond(v).wait_send()
        to_partner(v).wait_send()
        forward(v).wait_send()
        to_left(v).wait_send()
        to_right(v).wait_send()


def per_device(background, slab_owner, class_length_scale, band_widths, x_class, y_class, z_class):
    lx, ly, nslab = background.shape
    nvar, lev = z_class.shape
    size_x = lax.axis_size("sx")
    size_y = lax.axis_size("sy")
    span = lx + 2 * REACH
    vmem = pl.BlockSpec(memory_space=pltpu.VMEM)
    smem = pl.BlockSpec(memory_space=pltpu.SMEM)
    energy, cov = pl.pallas_call(
        functools.partial(kernel, size_x, size_y, lev),
        out_shape=(
            jax.ShapeDtypeStruct((nvar, lx, LANES), F32),
            jax.ShapeDtypeStruct((lx, ly, nslab), BF16),
        ),
        in_specs=[pl.BlockSpec(memory_space=pl.ANY), smem, smem, vmem, vmem, vmem],
        out_specs=(vmem, vmem),
        scratch_shapes=[
            pltpu.VMEM((lx, ly, nslab), BF16),
            pltpu.VMEM((nvar, span, ly, LANES), BF16),
            pltpu.VMEM((nvar, lx, ly + 2 * REACH, LANES), BF16),
            pltpu.VMEM((nvar, lx, ly, LANES), BF16),
            pltpu.VMEM((nvar, lx * PACK, span * PACK), BF16),
            pltpu.VMEM((nvar, ly, LANES), BF16),
            pltpu.VMEM((nvar, 2 * LANES, LANES), BF16),
            pltpu.VMEM((nvar, LANES, LANES), BF16),
            pltpu.VMEM((LANES, span * PACK), BF16),
            pltpu.VMEM((8, LANES), jnp.int32),
            pltpu.SemaphoreType.DMA,
            pltpu.SemaphoreType.DMA((nvar, 4)),
            pltpu.SemaphoreType.DMA((nvar, 4)),
            pltpu.SemaphoreType.DMA((nvar, 2)),
            pltpu.SemaphoreType.DMA((nvar, 2)),
        ],
        compiler_params=pltpu.CompilerParams(
            collective_id=0, has_side_effects=True, vmem_limit_bytes=60000 * 1024
        ),
    )(background, class_length_scale, band_widths, x_class, y_class, z_class)

    summed = energy[:, :, :lev].transpose(0, 2, 1).reshape(nslab, lx)
    slots = jnp.zeros((size_x * size_y, lx), F32).at[slab_owner].set(summed).reshape(size_x, size_y, lx)
    parts = lax.all_to_all(slots, "sy", split_axis=1, concat_axis=1, tiled=True)
    mine = jnp.sum(parts, 1)
    rows = lax.all_to_all(mine, "sx", split_axis=0, concat_axis=0, tiled=True)
    return rows.reshape(1, size_x * lx), cov


def solution(mesh):
    in_specs = (P("sx", "sy", None), P(), P(), P(), P(), P(), P())
    out_specs = (P(("sx", "sy"), None), P("sx", "sy", None))
    return jax.shard_map(per_device, mesh=mesh, in_specs=in_specs, out_specs=out_specs, check_vma=False)
```

time: 453 us -> 146 us (0.32); the launches traced: 446 us -> 145 us
  blocking collectives: 174 us -> 14.5 us
  waiting for transfers between devices: 147 us -> 9.3 us
  Pallas kernels: 0 us -> 97.4 us
  local copies, waits for them, and re-layouts: 90.5 us -> 9.85 us
  matrix products: 9.76 us -> 0 us
  starting transfers between devices: 16.4 us -> 11.4 us
  other arithmetic: 6.8 us -> 2.25 us
    all_to_all x2 -> x1, blocking collectives: 174 us -> 14.5 us  [per_device(): parts = lax.all_to_all(slots, 'sy', split_axis=1, concat_axis=1, tiled=True)]
    all_to_all x2 -> x1, waiting for transfers between devices: 147 us -> 9.3 us  [per_device(): rows = lax.all_to_all(mine, 'sx', split_axis=0, concat_axis=0, tiled=True)]
    pallas_call x0 -> x1, Pallas kernels: none -> 97.4 us  [per_device(): pl.pallas_call(functools.partial(kernel, size_x, size_y, lev), out_shape=...]
    reshape x6 -> x5, local copies, waits for them, and re-layouts: 22.3 us -> 1.17 us  [the longest x1 0.69 us: per_device(): return (rows.reshape(1, size_x * lx), cov)]
    another operation x3 -> x0, local copies, waits for them, and re-layouts: 16.4 us -> none  [the longest x1 8.36 us: filter_x(): windows = jnp.stack([padded[start:start + nblock] for start in range(3)])]
    gather x4 -> x0, local copies, waits for them, and re-layouts: 13.3 us -> none  [the longest x2 7.2 us: per_device(): jnp.take(extended, table, axis=0)]
    transpose x2, local copies, waits for them, and re-layouts: 13.1 us -> 1.06 us  [per_device(): summed = energy[:, :, :lev].transpose(0, 2, 1).reshape(nslab, lx)]
    dot_general x3 -> x0, matrix products: 9.76 us -> none  [the longest x1 4.67 us: filter_x(): jnp.einsum('obcy,obrc->bry', windows, weights, preferred_element_type=jnp...]
  transfers between devices with their start and end apart: 2 -> 1, of which waited for: 2 -> 1; matrix products, arithmetic and copies ran while one was open for 2% -> 0% of each run, Pallas kernels for 0% -> 0%
where the time goes in v1:
time: 146 us; the launch traced here: 145 us
  Pallas kernels  97.4 us (67%)
  blocking collectives  14.5 us (10%)
  starting transfers between devices  11.4 us (8%)
  local copies, waits for them, and re-layouts  9.85 us (7%)
  waiting for transfers between devices  9.3 us (6%)
  other arithmetic  2.25 us (2%)
    pallas_call x1, Pallas kernels, per_device(): pl.pallas_call(functools.partial(kernel, size_x, size_y, lev), out_shape=...  97.4 us
    all_to_all x1, blocking collectives, per_device(): parts = lax.all_to_all(slots, 'sy', split_axis=1, concat_axis=1, tiled=True)  14.5 us
    all_to_all x1, starting transfers between devices, per_device(): rows = lax.all_to_all(mine, 'sx', split_axis=0, concat_axis=0, tiled=True)  11.4 us
    all_to_all x1, waiting for transfers between devices, per_device(): rows = lax.all_to_all(mine, 'sx', split_axis=0, concat_axis=0, tiled=True)  9.3 us
    scatter x1, local copies, waits for them, and re-layouts, per_device(): jnp.zeros((size_x * size_y, lx), F32).at[slab_owner].set(summed)  4.26 us
  transfers between devices with their start and end apart: 1, of which 1 were waited for; matrix products, arithmetic and copies ran while one was open for 0% of the time, Pallas kernels for 0%

profile of v1, /device:TPU:1, one launch (start us, length us, event | category | flops | bytes accessed | tf_op | source)
XLA Modules:
  0.0 145.5 jit_solution(16464407358877661532)
XLA Ops:
  0.6 0.7 compare_select_fusion
  1.3 97.4 %shard_map.86 = (f32[6,24,128]{2,1,0:T(8,128)}, bf16[24,64,762]{2,1,0:T(8,128)(2,1)}) custom-call(bf16[24,64,762]{2,1,0:T(8,128)(2,1)} %background.1, f32[16]{0:T(128)} %scale_table.1, s32[16]{0:T(128)} %reach_table.1, s32[6,1536]{1,0:T(8,128)} %x_class.1, s32[6,768]{1,0:T(8,128)} %y_class.1, s32[6,127]{1,0:T(8,128)} %z_class.1), custom_call_target="tpu_custom_call" | custom-call | tf_op jit(solution)/shard_map/pallas_call | solution.py:289
  98.8 0.0 copy-start
  98.8 1.0 slice_bitcast_fusion
  99.8 0.1 reshape.23
  99.9 0.2 copy.14
  100.1 4.3 %scatter_custom_fusion = f32[768,24]{1,0:T(8,128)S(1)} fusion(s32[762]{0:T(1024)S(1)} %compare_select_fusion, f32[762,24]{1,0:T(8,128)S(1)} %copy.14, f32[]{:T(128)} %constant.3.clone.1), kind=kCustom, calls=%fused_computation.1 | custom fusion | bytes 73732 | tf_op jit(solution)/shard_map/scatter | solution.py:320
  104.4 0.2 copy.16
  104.6 0.1 reshape.40
  104.8 14.5 %all_to_all.14 = f32[12,1,1536]{2,1,0:T(1,128)S(1)} all-to-all(f32[12,1,1536]{2,1,0:T(1,128)S(1)} %reshape.40), channel_id=1, replica_groups=mesh['sx'=64,'sy'=12] {'sy'}, dimensions={0} | all-to-all | bytes 147456 | tf_op jit(solution)/shard_map/all_to_all | solution.py:321
  119.2 0.5 broadcast.4
  119.7 0.8 reduce.4
  120.6 0.1 reshape.41
  120.7 0.7 copy.18
  121.4 11.4 %all-to-all-start.1 = ((f32[64,1,24]{2,1,0:T(1,128)}), f32[64,1,24]{2,1,0:T(1,128)S(1)}, u32[]{:S(2)}, u32[]{:S(2)}) async-start(f32[64,1,24]{2,1,0:T(1,128)} %copy.18), calls=%async_computation.1 | async-start | bytes 65536 | tf_op jit(solution)/shard_map/all_to_all | solution.py:323
  132.8 9.3 %all-to-all-done.1 = f32[64,1,24]{2,1,0:T(1,128)S(1)} async-done(((f32[64,1,24]{2,1,0:T(1,128)}), f32[64,1,24]{2,1,0:T(1,128)S(1)}, u32[]{:S(2)}, u32[]{:S(2)}) %all-to-all-start.1) | async-done | bytes 6176 | tf_op jit(solution)/shard_map/all_to_all | solution.py:323
  142.1 0.5 broadcast.3
  142.6 0.7 reduce.3
  143.4 0.7 reshape.18
  144.1 0.0 copy-done
  144.1 1.4 copy.23
  (3 shorter events, 0.1 us)
Async XLA Ops:
  98.8 45.3 %copy-start = (bf16[24,64,762]{2,1,0:T(8,128)(2,1)S(1)}, bf16[24,64,762]{2,1,0:T(8,128)(2,1)}, u32[]{:S(2)}) copy-start(bf16[24,64,762]{2,1,0:T(8,128)(2,1)} %get-tuple-element.9) | copy-start | bytes 7022596
  121.4 20.8 %all-to-all-start.1 = ((f32[64,1,24]{2,1,0:T(1,128)}), f32[64,1,24]{2,1,0:T(1,128)S(1)}, u32[]{:S(2)}, u32[]{:S(2)}) async-start(f32[64,1,24]{2,1,0:T(1,128)} %copy.18), calls=%async_computation.1 | async-start | bytes 65536 | tf_op jit(solution)/shard_map/all_to_all | solution.py:323

commit v2 on v1

--- a/solution.py
+++ b/solution.py
@@ -10,7 +10,8 @@
 MESH = pl.DeviceIdType.MESH
 REACH = 32
 LANES = 128
-PACK = 16
+PACK = 8
+GROUPS = ((0, 3), (3, 5), (5, 6))
 F32 = jnp.float32
 BF16 = jnp.bfloat16
 
@@ -56,6 +57,7 @@
     size_y,
     lev,
     background,
+    slab_owner,
     scale_table,
     reach_table,
     x_class,
@@ -73,11 +75,24 @@
     wxt,
     spread,
     tables,
+    cov,
+    onehot,
+    mine,
+    others,
+    rows_out,
+    rows_in,
+    table,
+    fill,
     raw_sem,
+    cov_sem,
     near_send,
     near_recv,
     side_send,
     side_recv,
+    sum_send,
+    sum_recv,
+    row_send,
+    row_recv,
 ):
     lx, ly, nslab = background.shape
     nvar = z_class.shape[0]
@@ -96,8 +111,14 @@
     load = pltpu.make_async_copy(background, raw, raw_sem)
     load.start()
     barrier = pltpu.get_barrier_semaphore()
-    for peer in (at_x(-2), at_x(-1), at_x(1), at_x(2), at_y(-1), at_y(1)):
-        pl.semaphore_signal(barrier, inc=1, device_id=peer, device_id_type=MESH)
+
+    @pl.loop(1, size_y)
+    def _(k):
+        pl.semaphore_signal(barrier, inc=1, device_id=at_y(k), device_id_type=MESH)
+
+    @pl.loop(1, size_x)
+    def _(k):
+        pl.semaphore_signal(barrier, inc=1, device_id=at_x(k), device_id_type=MESH)
 
     outer = at_x(2 * core - 1)
     partner = at_x(1 - 2 * core)
@@ -109,20 +130,20 @@
         )
 
     def to_outer(v):
-        own = win.at[v, pl.ds(REACH, lx)]
-        return remote(own, win.at[v, pl.ds(REACH + lx - 2 * lx * core, lx)], near_send.at[v, 0], near_recv.at[v, 0], outer)
+        own = win.at[v, :, pl.ds(REACH, lx)]
+        return remote(own, win.at[v, :, pl.ds(REACH + lx - 2 * lx * core, lx)], near_send.at[v, 0], near_recv.at[v, 0], outer)
 
     def to_partner(v):
-        own = win.at[v, pl.ds(REACH, lx)]
-        return remote(own, win.at[v, pl.ds(far + 2 * lx * core, lx)], near_send.at[v, 1], near_recv.at[v, 1], partner)
+        own = win.at[v, :, pl.ds(REACH, lx)]
+        return remote(own, win.at[v, :, pl.ds(far + 2 * lx * core, lx)], near_send.at[v, 1], near_recv.at[v, 1], partner)
 
     def to_beyond(v):
-        own = win.at[v, pl.ds(REACH + (lx - far) * (1 - core), far)]
-        return remote(own, win.at[v, pl.ds((span - far) * core, far)], near_send.at[v, 2], near_recv.at[v, 2], beyond)
+        own = win.at[v, :, pl.ds(REACH + (lx - far) * (1 - core), far)]
+        return remote(own, win.at[v, :, pl.ds((span - far) * core, far)], near_send.at[v, 2], near_recv.at[v, 2], beyond)
 
     def forward(v):
-        got = win.at[v, pl.ds(far + (lx - far) + REACH * core, far)]
-        return remote(got, win.at[v, pl.ds((span - far) * core, far)], near_send.at[v, 3], near_recv.at[v, 3], partner)
+        got = win.at[v, :, pl.ds(far + (lx - far) + REACH * core, far)]
+        return remote(got, win.at[v, :, pl.ds((span - far) * core, far)], near_send.at[v, 3], near_recv.at[v, 3], partner)
 
     def to_left(v):
         own = xfw.at[v, :, pl.ds(REACH, REACH)]
@@ -133,14 +154,28 @@
         return remote(own, xfw.at[v, :, pl.ds(0, REACH)], side_send.at[v, 1], side_recv.at[v, 1], at_y(1))
 
     def align(v):
-        @pl.loop(0, lx)
-        def _(i):
-            win[v, REACH + i] = jnp.zeros((ly, LANES), BF16)
-            win[v, REACH + i, :, 0:lev] = raw[i, :, lev * v : lev * v + lev]
+        rows = 4
+        column = iota((ly, LANES), 1)
+
+        @pl.loop(0, lx // rows)
+        def _(block):
+            for r in range(rows):
+                i = block * rows + r
+                if LANES * (v + 1) > nslab:
+                    win[v, :, REACH + i] = jnp.zeros((ly // PACK, PACK, LANES), BF16)
+                    piece = raw[i, :, lev * v : lev * (v + 1)]
+                    win[v, :, REACH + i, :, 0:lev] = piece.reshape(ly // PACK, PACK, lev)
+                    continue
+                tile = raw[i, :, LANES * v : LANES * (v + 1)].astype(F32)
+                if v > 0:
+                    before = raw[i, :, LANES * (v - 1) : LANES * v].astype(F32)
+                    tile = pltpu.roll(jnp.where(column >= LANES - v, before, tile), v, 1)
+                tile = jnp.where(column < lev, tile, 0.0).astype(BF16)
+                win[v, :, REACH + i] = tile.reshape(ly // PACK, PACK, LANES)
 
     load.wait()
     align(0)
-    pl.semaphore_wait(barrier, 6)
+    pl.semaphore_wait(barrier, size_x + size_y - 2)
     for v in range(nvar):
         if v + 1 < nvar:
             align(v + 1)
@@ -174,12 +209,12 @@
         wy[v] = dot_nt(eye, jnp.where(lane < ly, weight, 0.0).astype(BF16)).astype(BF16)
 
     spread[...] = (iota(spread.shape, 1) // PACK == iota(spread.shape, 0)).astype(BF16)
-    part = lx * PACK // 4
-
-    @pl.loop(0, nvar * 4)
+    part = lx * PACK // 2
+
+    @pl.loop(0, nvar * 2)
     def _(step):
-        v = step // 4
-        first = pl.multiple_of((step % 4) * part, 16)
+        v = step // 2
+        first = pl.multiple_of((step % 2) * part, 16)
         row = iota((part, LANES), 0) + first
         pick = (row // PACK == iota((part, LANES), 1)).astype(BF16)
         rows = dot_nt(pick, wxt[v]).astype(BF16)
@@ -209,30 +244,44 @@
             lower = normalised(bump_of(offset_z, inside, scale_z))
             wz[t, LANES : 2 * LANES] = jnp.where(lane >= lev - t, lower, 0.0).astype(BF16)
 
+    for v in range(nvar):
+        fill[...] = jnp.full(fill.shape, -1, jnp.int32)
+        fill[0:1, 0:lev] = slab_owner[:, lev * v : lev * (v + 1)]
+        owner = fill[0:1, :]
+        owner_x = (owner * ((1 << 19) // size_y + 1)) >> 19
+        owner_y = owner - owner_x * size_y
+        match = (iota((onehot.shape[1], LANES), 0) == owner_x) & (owner_y == q) & (owner >= 0)
+        onehot[v] = match.astype(BF16)
+    n_out = size_x * lx
+    table[...] = (iota(table.shape, 1) % lx == iota(table.shape, 0)).astype(BF16)
+
     def filter_x(v):
-        @pl.loop(0, ly // (2 * PACK))
-        def _(half):
-            first = pl.multiple_of(half * 2 * PACK, 2 * PACK)
-            left = win[v, :, pl.ds(first, PACK), :].reshape(span * PACK, LANES)
-            right = win[v, :, pl.ds(first + PACK, PACK), :].reshape(span * PACK, LANES)
-            got = dot_nn(kron[v], jnp.concatenate([left, right], 1)).astype(BF16)
-            got = got.reshape(lx, PACK, 2 * LANES)
-            xfw[v, :, pl.ds(first + REACH, PACK), :] = got[:, :, 0:LANES]
-            xfw[v, :, pl.ds(first + REACH + PACK, PACK), :] = got[:, :, LANES:]
+        wide = 4
+
+        @pl.loop(0, ly // (wide * PACK))
+        def _(part):
+            blocks = [win[v, wide * part + k].reshape(span * PACK, LANES) for k in range(wide)]
+            got = dot_nn(kron[v], jnp.concatenate(blocks, 1)).reshape(lx, PACK, wide * LANES)
+            for k in range(wide):
+                first = pl.multiple_of((wide * part + k) * PACK + REACH, PACK)
+                xfw[v, :, pl.ds(first, PACK), :] = got[:, :, LANES * k : LANES * (k + 1)].astype(BF16)
 
     def filter_y(v):
-        @pl.loop(0, lx // 2)
-        def _(pair):
-            both = jnp.concatenate([xfw[v, 2 * pair], xfw[v, 2 * pair + 1]], 1)
-            got = dot_nn(wy[v], both)
-            power = jnp.sum(got * got, 0, keepdims=True)
-            for k in range(2):
-                piece = got[:, LANES * k : LANES * (k + 1)]
-                yr[v, 2 * pair + k] = piece.astype(BF16)
-                energy_out[v, pl.ds(2 * pair + k, 1), :] = power[:, LANES * k : LANES * (k + 1)]
+        rows = 12
+
+        @pl.loop(0, lx // rows)
+        def _(block):
+            for r in range(0, rows, 2):
+                i = block * rows + r
+                both = jnp.concatenate([xfw[v, i], xfw[v, i + 1]], 1)
+                got = dot_nn(wy[v], both)
+                power = jnp.sum(got * got, 0, keepdims=True)
+                for k in range(2):
+                    yr[v, i + k] = got[:, LANES * k : LANES * (k + 1)].astype(BF16)
+                    mine[v, pl.ds(i + k, 1), :] = power[:, LANES * k : LANES * (k + 1)]
 
     def filter_z(t):
-        rows = 4
+        rows = 8
         width = min(LANES, nslab - LANES * t)
 
         @pl.loop(0, lx // rows)
@@ -245,30 +294,81 @@
             else:
                 got = dot_nn(here, wz[t, 0:LANES])
             got = got.astype(BF16).reshape(rows, ly, LANES)
-            cov_out[pl.ds(first, rows), :, LANES * t : LANES * t + width] = got[:, :, 0:width]
-
+            cov[pl.ds(first, rows), :, LANES * t : LANES * t + width] = got[:, :, 0:width]
+
+    def tell(g, k):
+        part = pl.ds(GROUPS[g][0], GROUPS[g][1] - GROUPS[g][0])
+        return remote(mine.at[part], others.at[k, part], sum_send.at[g, k], sum_recv.at[g, k], at_y(k))
+
+    def tell_all(g):
+        @pl.loop(1, size_y)
+        def _(k):
+            tell(g, k).start()
+
+    def hand(k):
+        to = lax.rem(p + k, size_x)
+        return remote(rows_out.at[to], rows_in.at[p], row_send.at[k], row_recv.at[k], (to, q))
+
+    last_of = {stop - 1: g for g, (_, stop) in enumerate(GROUPS)}
     for v in range(nvar):
         to_outer(v).wait_recv()
         forward(v).start()
         to_beyond(v).wait_recv()
         to_partner(v).wait_recv()
+        forward(v).wait_recv()
+        filter_x(v)
+        to_left(v).start()
+        to_right(v).start()
         if v >= 1:
             to_left(v - 1).wait_recv()
             to_right(v - 1).wait_recv()
             filter_y(v - 1)
+            if v - 1 in last_of:
+                tell_all(last_of[v - 1])
         if v >= 2:
             filter_z(v - 2)
-        forward(v).wait_recv()
-        filter_x(v)
-        to_left(v).start()
-        to_right(v).start()
     v = nvar - 1
     to_left(v).wait_recv()
     to_right(v).wait_recv()
     filter_y(v)
+    tell_all(last_of[v])
     filter_z(v - 1)
     filter_z(v)
-
+    store = pltpu.make_async_copy(cov, cov_out, cov_sem)
+    store.start()
+
+    for g in range(len(GROUPS)):
+        @pl.loop(1, size_y)
+        def _(k):
+            tell(g, k).wait()
+    picked = jnp.zeros((onehot.shape[1], lx), F32)
+    for v in range(nvar):
+        total = mine[v]
+        for k in range(1, size_y):
+            total = total + others[k, v]
+        for piece in split3(total):
+            picked = picked + dot_nt(onehot[v], piece)
+    fill_rows = picked.reshape(onehot.shape[1], 1, lx)
+    rows_out[:, :, 0:lx] = fill_rows
+    rows_in[p, :, 0:lx] = rows_out[p, :, 0:lx]
+
+    @pl.loop(1, size_x)
+    def _(k):
+        hand(k).start()
+
+    @pl.loop(1, size_x)
+    def _(k):
+        hand(k).wait()
+    arrived = rows_in[:, :, 0:lx].reshape(size_x, lx)
+    home = (iota((size_x, n_out), 1) >= lx * iota((size_x, n_out), 0)) & (
+        iota((size_x, n_out), 1) < lx * iota((size_x, n_out), 0) + lx
+    )
+    spread_rows = jnp.zeros((size_x, n_out), F32)
+    for piece in split3(arrived):
+        spread_rows = spread_rows + dot_nn(piece, table[...])
+    energy_out[...] = jnp.sum(jnp.where(home, spread_rows, 0.0), 0, keepdims=True)
+
+    store.wait()
     for v in range(nvar):
         to_outer(v).wait_send()
         to_beyond(v).wait_send()
@@ -289,14 +389,14 @@
     energy, cov = pl.pallas_call(
         functools.partial(kernel, size_x, size_y, lev),
         out_shape=(
-            jax.ShapeDtypeStruct((nvar, lx, LANES), F32),
+            jax.ShapeDtypeStruct((1, size_x * lx), F32),
             jax.ShapeDtypeStruct((lx, ly, nslab), BF16),
         ),
-        in_specs=[pl.BlockSpec(memory_space=pl.ANY), smem, smem, vmem, vmem, vmem],
-        out_specs=(vmem, vmem),
+        in_specs=[pl.BlockSpec(memory_space=pl.ANY), vmem, smem, smem, vmem, vmem, vmem],
+        out_specs=(vmem, pl.BlockSpec(memory_space=pl.ANY)),
         scratch_shapes=[
             pltpu.VMEM((lx, ly, nslab), BF16),
-            pltpu.VMEM((nvar, span, ly, LANES), BF16),
+            pltpu.VMEM((nvar, ly // PACK, span, PACK, LANES), BF16),
             pltpu.VMEM((nvar, lx, ly + 2 * REACH, LANES), BF16),
             pltpu.VMEM((nvar, lx, ly, LANES), BF16),
             pltpu.VMEM((nvar, lx * PACK, span * PACK), BF16),
@@ -305,23 +405,30 @@
             pltpu.VMEM((nvar, LANES, LANES), BF16),
             pltpu.VMEM((LANES, span * PACK), BF16),
             pltpu.VMEM((8, LANES), jnp.int32),
+            pltpu.VMEM((lx, ly, nslab), BF16),
+            pltpu.VMEM((nvar, size_x, LANES), BF16),
+            pltpu.VMEM((nvar, lx, LANES), F32),
+            pltpu.VMEM((size_y, nvar, lx, LANES), F32),
+            pltpu.VMEM((size_x, 1, LANES), F32),
+            pltpu.VMEM((size_x, 1, LANES), F32),
+            pltpu.VMEM((lx, size_x * lx), BF16),
+            pltpu.VMEM((8, LANES), jnp.int32),
+            pltpu.SemaphoreType.DMA,
             pltpu.SemaphoreType.DMA,
             pltpu.SemaphoreType.DMA((nvar, 4)),
             pltpu.SemaphoreType.DMA((nvar, 4)),
             pltpu.SemaphoreType.DMA((nvar, 2)),
             pltpu.SemaphoreType.DMA((nvar, 2)),
+            pltpu.SemaphoreType.DMA((len(GROUPS), size_y)),
+            pltpu.SemaphoreType.DMA((len(GROUPS), size_y)),
+            pltpu.SemaphoreType.DMA((size_x,)),
+            pltpu.SemaphoreType.DMA((size_x,)),
         ],
         compiler_params=pltpu.CompilerParams(
             collective_id=0, has_side_effects=True, vmem_limit_bytes=60000 * 1024
         ),
-    )(background, class_length_scale, band_widths, x_class, y_class, z_class)
-
-    summed = energy[:, :, :lev].transpose(0, 2, 1).reshape(nslab, lx)
-    slots = jnp.zeros((size_x * size_y, lx), F32).at[slab_owner].set(summed).reshape(size_x, size_y, lx)
-    parts = lax.all_to_all(slots, "sy", split_axis=1, concat_axis=1, tiled=True)
-    mine = jnp.sum(parts, 1)
-    rows = lax.all_to_all(mine, "sx", split_axis=0, concat_axis=0, tiled=True)
-    return rows.reshape(1, size_x * lx), cov
+    )(background, slab_owner.reshape(1, nslab), class_length_scale, band_widths, x_class, y_class, z_class)
+    return energy, cov
 
 
 def solution(mesh):

time: 146 us -> 114 us (0.78)
  blocking collectives: 14.5 us -> 0 us
  starting transfers between devices: 11.4 us -> 0 us
  Pallas kernels: 97.4 us -> 107 us
  waiting for transfers between devices: 9.3 us -> 0 us
  local copies, waits for them, and re-layouts: 9.85 us -> 5.85 us
  other arithmetic: 2.25 us -> 0 us
    all_to_all x1 -> x0, blocking collectives: 14.5 us -> none  [per_device(): parts = lax.all_to_all(slots, 'sy', split_axis=1, concat_axis=1, tiled=True)]
    all_to_all x1 -> x0, starting transfers between devices: 11.4 us -> none  [per_device(): rows = lax.all_to_all(mine, 'sx', split_axis=0, concat_axis=0, tiled=True)]
    pallas_call x1, Pallas kernels: 97.4 us -> 107 us  [per_device(): pl.pallas_call(functools.partial(kernel, size_x, size_y, lev), out_shape=...]
    all_to_all x1 -> x0, waiting for transfers between devices: 9.3 us -> none  [per_device(): rows = lax.all_to_all(mine, 'sx', split_axis=0, concat_axis=0, tiled=True)]
    scatter x1 -> x0, local copies, waits for them, and re-layouts: 4.26 us -> none  [per_device(): jnp.zeros((size_x * size_y, lx), F32).at[slab_owner].set(summed)]
    unnamed x5 -> x2, local copies, waits for them, and re-layouts: 1.63 us -> 4.58 us
    all_to_all x3 -> x0, local copies, waits for them, and re-layouts: 1.72 us -> none  [the longest x2 1.21 us: per_device(): rows = lax.all_to_all(mine, 'sx', split_axis=0, concat_axis=0, tiled=True)]
    all_to_all x2 -> x0, other arithmetic: 1.54 us -> none  [the longest x1 0.82 us: per_device(): parts = lax.all_to_all(slots, 'sy', split_axis=1, concat_axis=1, tiled=True)]
  transfers between devices with their start and end apart: 1 -> 0, of which waited for: 1 -> 0; matrix products, arithmetic and copies ran while one was open for 0% -> 0% of each run, Pallas kernels for 0% -> 0%
where the time goes in v2:
time: 114 us; the launch traced here: 113 us
  Pallas kernels  107 us (94%)
  local copies, waits for them, and re-layouts  5.85 us (5%)
    pallas_call x1, Pallas kernels, per_device(): pl.pallas_call(functools.partial(kernel, size_x, size_y, lev), out_shape=...  107 us
    unnamed x2, local copies, waits for them, and re-layouts  4.58 us

profile of v2, /device:TPU:1, one launch (start us, length us, event | category | flops | bytes accessed | tf_op | source)
XLA Modules:
  0.0 113.5 jit_solution(13918874164399379431)
XLA Ops:
  0.6 1.3 %reshape.7.slab_owner = s32[1,762]{1,0:T(1,128)} reshape(s32[762]{0:T(1024)} %param.8) | data formatting | bytes 6096 | tf_op jit(solution)/shard_map/reshape | solution.py:430
  1.9 107.0 %shard_map.86 = (f32[1,1536]{1,0:T(1,128)}, bf16[24,64,762]{2,1,0:T(8,128)(2,1)}) custom-call(bf16[24,64,762]{2,1,0:T(8,128)(2,1)} %background.1, s32[1,762]{1,0:T(1,128)} %reshape.7.slab_owner, f32[16]{0:T(128)} %scale_table.1, s32[16]{0:T(128)} %reach_table.1, s32[6,1536]{1,0:T(8,128)} %x_class.1, s32[6,768]{1,0:T(8,128)} %y_class.1, s32[6,127]{1,0:T(8,128)} %z_class.1), custom_call_target="tpu_custom_call" | custom-call | tf_op jit(solution)/shard_map/pallas_call | solution.py:389
  108.9 1.3 %copy.11 = f32[1,1536]{1,0:T(1,128)} copy(f32[1,1536]{1,0:T(1,128)} %get-tuple-element.4) | data formatting | bytes 12288
  110.2 3.3 %copy.12 = bf16[24,64,762]{2,1,0:T(8,128)(2,1)} copy(bf16[24,64,762]{2,1,0:T(8,128)(2,1)} %get-tuple-element.5) | data formatting | bytes 4681728

commit v3 on v2

--- a/solution.py
+++ b/solution.py
@@ -11,7 +11,8 @@
 REACH = 32
 LANES = 128
 PACK = 8
-GROUPS = ((0, 3), (3, 5), (5, 6))
+HALF = 12
+STEP = 16
 F32 = jnp.float32
 BF16 = jnp.bfloat16
 
@@ -65,6 +66,7 @@
     z_class,
     energy_out,
     cov_out,
+    first_tile,
     raw,
     win,
     xfw,
@@ -75,16 +77,17 @@
     wxt,
     spread,
     tables,
-    cov,
     onehot,
     mine,
-    others,
+    slots,
+    outbox,
+    inbox,
     rows_out,
     rows_in,
     table,
     fill,
+    first_sem,
     raw_sem,
-    cov_sem,
     near_send,
     near_recv,
     side_send,
@@ -101,6 +104,7 @@
     p = lax.axis_index("sx")
     q = lax.axis_index("sy")
     core = lax.rem(p, 2)
+    unroll_x = 7 if size_x % 7 == 1 else 1
 
     def at_x(step):
         return (lax.rem(p + step + size_x, size_x), q)
@@ -108,15 +112,17 @@
     def at_y(step):
         return (p, lax.rem(q + step + size_y, size_y))
 
+    load_first = pltpu.make_async_copy(background.at[:, :, 0:LANES], first_tile, first_sem)
+    load_first.start()
     load = pltpu.make_async_copy(background, raw, raw_sem)
     load.start()
     barrier = pltpu.get_barrier_semaphore()
 
-    @pl.loop(1, size_y)
+    @pl.loop(1, size_y, unroll=True)
     def _(k):
         pl.semaphore_signal(barrier, inc=1, device_id=at_y(k), device_id_type=MESH)
 
-    @pl.loop(1, size_x)
+    @pl.loop(1, size_x, unroll=unroll_x)
     def _(k):
         pl.semaphore_signal(barrier, inc=1, device_id=at_x(k), device_id_type=MESH)
 
@@ -166,22 +172,25 @@
                     piece = raw[i, :, lev * v : lev * (v + 1)]
                     win[v, :, REACH + i, :, 0:lev] = piece.reshape(ly // PACK, PACK, lev)
                     continue
-                tile = raw[i, :, LANES * v : LANES * (v + 1)].astype(F32)
+                tile = (first_tile[i] if v == 0 else raw[i, :, LANES * v : LANES * (v + 1)]).astype(F32)
                 if v > 0:
                     before = raw[i, :, LANES * (v - 1) : LANES * v].astype(F32)
                     tile = pltpu.roll(jnp.where(column >= LANES - v, before, tile), v, 1)
                 tile = jnp.where(column < lev, tile, 0.0).astype(BF16)
                 win[v, :, REACH + i] = tile.reshape(ly // PACK, PACK, LANES)
 
-    load.wait()
+    load_first.wait()
     align(0)
     pl.semaphore_wait(barrier, size_x + size_y - 2)
     for v in range(nvar):
-        if v + 1 < nvar:
-            align(v + 1)
         to_outer(v).start()
         to_beyond(v).start()
         to_partner(v).start()
+        if v == 0:
+            load.wait()
+            align(1)
+        if v + 2 < nvar:
+            align(v + 2)
 
     n_x = size_x * lx
     n_y = size_y * ly
@@ -244,16 +253,20 @@
             lower = normalised(bump_of(offset_z, inside, scale_z))
             wz[t, LANES : 2 * LANES] = jnp.where(lane >= lev - t, lower, 0.0).astype(BF16)
 
-    for v in range(nvar):
-        fill[...] = jnp.full(fill.shape, -1, jnp.int32)
-        fill[0:1, 0:lev] = slab_owner[:, lev * v : lev * (v + 1)]
-        owner = fill[0:1, :]
+    fill[...] = jnp.full(fill.shape, -1, jnp.int32)
+    for v in range(nvar):
+        fill[v : v + 1, 0:lev] = slab_owner[lev * v : lev * (v + 1)].reshape(1, lev)
+    for v in range(nvar):
+        owner = fill[v : v + 1, :]
         owner_x = (owner * ((1 << 19) // size_y + 1)) >> 19
-        owner_y = owner - owner_x * size_y
-        match = (iota((onehot.shape[1], LANES), 0) == owner_x) & (owner_y == q) & (owner >= 0)
-        onehot[v] = match.astype(BF16)
+        place = jnp.where(owner >= 0, owner_x + LANES * (owner - owner_x * size_y), -1)
+        onehot[v] = (iota((size_y * LANES, LANES), 0) == place).astype(BF16)
     n_out = size_x * lx
-    table[...] = (iota(table.shape, 1) % lx == iota(table.shape, 0)).astype(BF16)
+    cell = iota(table.shape, 1) % lx
+    table[...] = (cell + (STEP - HALF) * (cell // HALF) == iota(table.shape, 0)).astype(BF16)
+    mine[...] = jnp.zeros(mine.shape, F32)
+    rows_out[...] = jnp.zeros(rows_out.shape, F32)
+    eye_x = (iota((size_x, LANES), 0) == iota((size_x, LANES), 1)).astype(BF16)
 
     def filter_x(v):
         wide = 4
@@ -267,7 +280,7 @@
                 xfw[v, :, pl.ds(first, PACK), :] = got[:, :, LANES * k : LANES * (k + 1)].astype(BF16)
 
     def filter_y(v):
-        rows = 12
+        rows = HALF
 
         @pl.loop(0, lx // rows)
         def _(block):
@@ -278,7 +291,7 @@
                 power = jnp.sum(got * got, 0, keepdims=True)
                 for k in range(2):
                     yr[v, i + k] = got[:, LANES * k : LANES * (k + 1)].astype(BF16)
-                    mine[v, pl.ds(i + k, 1), :] = power[:, LANES * k : LANES * (k + 1)]
+                    mine[v, pl.ds(block * STEP + r + k, 1), :] = power[:, LANES * k : LANES * (k + 1)]
 
     def filter_z(t):
         rows = 8
@@ -294,22 +307,25 @@
             else:
                 got = dot_nn(here, wz[t, 0:LANES])
             got = got.astype(BF16).reshape(rows, ly, LANES)
-            cov[pl.ds(first, rows), :, LANES * t : LANES * t + width] = got[:, :, 0:width]
-
-    def tell(g, k):
-        part = pl.ds(GROUPS[g][0], GROUPS[g][1] - GROUPS[g][0])
-        return remote(mine.at[part], others.at[k, part], sum_send.at[g, k], sum_recv.at[g, k], at_y(k))
-
-    def tell_all(g):
-        @pl.loop(1, size_y)
-        def _(k):
-            tell(g, k).start()
+            cov_out[pl.ds(first, rows), :, LANES * t : LANES * t + width] = got[:, :, 0:width]
+
+    def gather_slots(v):
+        got = dot_nt(jnp.concatenate(split3(mine[v]), 0), onehot[v])
+        rows = mine.shape[1]
+        got = got[0:rows] + got[rows : 2 * rows] + got[2 * rows :]
+        if v == 0:
+            slots[...] = got
+        else:
+            slots[...] += got
+
+    def tell(k):
+        to = lax.rem(q + k, size_y)
+        return remote(outbox.at[to], inbox.at[k], sum_send.at[k], sum_recv.at[k], (p, to))
 
     def hand(k):
         to = lax.rem(p + k, size_x)
         return remote(rows_out.at[to], rows_in.at[p], row_send.at[k], row_recv.at[k], (to, q))
 
-    last_of = {stop - 1: g for g, (_, stop) in enumerate(GROUPS)}
     for v in range(nvar):
         to_outer(v).wait_recv()
         forward(v).start()
@@ -323,52 +339,56 @@
             to_left(v - 1).wait_recv()
             to_right(v - 1).wait_recv()
             filter_y(v - 1)
-            if v - 1 in last_of:
-                tell_all(last_of[v - 1])
+            gather_slots(v - 1)
         if v >= 2:
             filter_z(v - 2)
     v = nvar - 1
     to_left(v).wait_recv()
     to_right(v).wait_recv()
     filter_y(v)
-    tell_all(last_of[v])
+    gather_slots(v)
+    for to in range(size_y):
+        block = slots[:, LANES * to : LANES * (to + 1)]
+        outbox[to] = block[0:STEP] + pltpu.roll(block[STEP : 2 * STEP], LANES // 2, 1)
+
+    @pl.loop(1, size_y, unroll=True)
+    def _(k):
+        tell(k).start()
+
     filter_z(v - 1)
     filter_z(v)
-    store = pltpu.make_async_copy(cov, cov_out, cov_sem)
-    store.start()
-
-    for g in range(len(GROUPS)):
-        @pl.loop(1, size_y)
-        def _(k):
-            tell(g, k).wait()
-    picked = jnp.zeros((onehot.shape[1], lx), F32)
-    for v in range(nvar):
-        total = mine[v]
-        for k in range(1, size_y):
-            total = total + others[k, v]
-        for piece in split3(total):
-            picked = picked + dot_nt(onehot[v], piece)
-    fill_rows = picked.reshape(onehot.shape[1], 1, lx)
-    rows_out[:, :, 0:lx] = fill_rows
-    rows_in[p, :, 0:lx] = rows_out[p, :, 0:lx]
-
-    @pl.loop(1, size_x)
+
+    @pl.loop(1, size_y, unroll=True)
+    def _(k):
+        tell(k).wait()
+
+    total = outbox[q]
+    for k in range(1, size_y):
+        total = total + inbox[k]
+    both = jnp.concatenate([total, pltpu.roll(total, LANES // 2, 1)], 0)
+    picked = jnp.zeros((size_x, 2 * STEP), F32)
+    for piece in split3(both):
+        picked = picked + dot_nt(eye_x, piece)
+    rows_out[:, :, 0 : 2 * STEP] = picked.reshape(size_x, 1, 2 * STEP)
+
+    @pl.loop(1, size_x, unroll=unroll_x)
     def _(k):
         hand(k).start()
 
-    @pl.loop(1, size_x)
+    rows_in[p] = rows_out[p]
+
+    @pl.loop(1, size_x, unroll=unroll_x)
     def _(k):
         hand(k).wait()
-    arrived = rows_in[:, :, 0:lx].reshape(size_x, lx)
-    home = (iota((size_x, n_out), 1) >= lx * iota((size_x, n_out), 0)) & (
-        iota((size_x, n_out), 1) < lx * iota((size_x, n_out), 0) + lx
-    )
-    spread_rows = jnp.zeros((size_x, n_out), F32)
-    for piece in split3(arrived):
-        spread_rows = spread_rows + dot_nn(piece, table[...])
-    energy_out[...] = jnp.sum(jnp.where(home, spread_rows, 0.0), 0, keepdims=True)
-
-    store.wait()
+
+    arrived = rows_in[:, :, 0 : 2 * STEP].reshape(size_x, 2 * STEP)
+    column = iota((size_x, n_out), 1)
+    start = lx * iota((size_x, n_out), 0)
+    home = (column >= start) & (column < start + lx)
+    wide_rows = dot_nn(jnp.concatenate(split3(arrived), 0), table[...])
+    wide_rows = wide_rows[0:size_x] + wide_rows[size_x : 2 * size_x] + wide_rows[2 * size_x :]
+    energy_out[...] = jnp.sum(jnp.where(home, wide_rows, 0.0), 0, keepdims=True)
+
     for v in range(nvar):
         to_outer(v).wait_send()
         to_beyond(v).wait_send()
@@ -389,12 +409,13 @@
     energy, cov = pl.pallas_call(
         functools.partial(kernel, size_x, size_y, lev),
         out_shape=(
-            jax.ShapeDtypeStruct((1, size_x * lx), F32),
-            jax.ShapeDtypeStruct((lx, ly, nslab), BF16),
+            pltpu.VMEM((1, size_x * lx), F32),
+            pltpu.VMEM((lx, ly, nslab), BF16),
         ),
         in_specs=[pl.BlockSpec(memory_space=pl.ANY), vmem, smem, smem, vmem, vmem, vmem],
-        out_specs=(vmem, pl.BlockSpec(memory_space=pl.ANY)),
+        out_specs=(vmem, vmem),
         scratch_shapes=[
+            pltpu.VMEM((lx, ly, LANES), BF16),
             pltpu.VMEM((lx, ly, nslab), BF16),
             pltpu.VMEM((nvar, ly // PACK, span, PACK, LANES), BF16),
             pltpu.VMEM((nvar, lx, ly + 2 * REACH, LANES), BF16),
@@ -405,13 +426,14 @@
             pltpu.VMEM((nvar, LANES, LANES), BF16),
             pltpu.VMEM((LANES, span * PACK), BF16),
             pltpu.VMEM((8, LANES), jnp.int32),
-            pltpu.VMEM((lx, ly, nslab), BF16),
-            pltpu.VMEM((nvar, size_x, LANES), BF16),
-            pltpu.VMEM((nvar, lx, LANES), F32),
-            pltpu.VMEM((size_y, nvar, lx, LANES), F32),
+            pltpu.VMEM((nvar, size_y * LANES, LANES), BF16),
+            pltpu.VMEM((nvar, 2 * STEP, LANES), F32),
+            pltpu.VMEM((2 * STEP, size_y * LANES), F32),
+            pltpu.VMEM((size_y, STEP, LANES), F32),
+            pltpu.VMEM((size_y, STEP, LANES), F32),
             pltpu.VMEM((size_x, 1, LANES), F32),
             pltpu.VMEM((size_x, 1, LANES), F32),
-            pltpu.VMEM((lx, size_x * lx), BF16),
+            pltpu.VMEM((2 * STEP, size_x * lx), BF16),
             pltpu.VMEM((8, LANES), jnp.int32),
             pltpu.SemaphoreType.DMA,
             pltpu.SemaphoreType.DMA,
@@ -419,15 +441,15 @@
             pltpu.SemaphoreType.DMA((nvar, 4)),
             pltpu.SemaphoreType.DMA((nvar, 2)),
             pltpu.SemaphoreType.DMA((nvar, 2)),
-            pltpu.SemaphoreType.DMA((len(GROUPS), size_y)),
-            pltpu.SemaphoreType.DMA((len(GROUPS), size_y)),
+            pltpu.SemaphoreType.DMA((size_y,)),
+            pltpu.SemaphoreType.DMA((size_y,)),
             pltpu.SemaphoreType.DMA((size_x,)),
             pltpu.SemaphoreType.DMA((size_x,)),
         ],
         compiler_params=pltpu.CompilerParams(
             collective_id=0, has_side_effects=True, vmem_limit_bytes=60000 * 1024
         ),
-    )(background, slab_owner.reshape(1, nslab), class_length_scale, band_widths, x_class, y_class, z_class)
+    )(background, slab_owner, class_length_scale, band_widths, x_class, y_class, z_class)
     return energy, cov
 
 

time: 114 us -> 86.6 us (0.76)
  Pallas kernels: 107 us -> 83.8 us
  local copies, waits for them, and re-layouts: 5.85 us -> 2 us
    pallas_call x1, Pallas kernels: 107 us -> 83.8 us  [per_device(): pl.pallas_call(functools.partial(kernel, size_x, size_y, lev), out_shape=...]
    unnamed x2, local copies, waits for them, and re-layouts: 4.58 us -> 2 us
    reshape x1 -> x0, local copies, waits for them, and re-layouts: 1.27 us -> none  [per_device(): slab_owner.reshape(1, nslab)]
where the time goes in v3:
time: 86.6 us; the launch traced here: 86.4 us
  Pallas kernels  83.8 us (97%)
  local copies, waits for them, and re-layouts  2 us (2%)
    pallas_call x1, Pallas kernels, per_device(): pl.pallas_call(functools.partial(kernel, size_x, size_y, lev), out_shape=...  83.8 us
    unnamed x2, local copies, waits for them, and re-layouts  2 us

profile of v3, /device:TPU:1, one launch (start us, length us, event | category | flops | bytes accessed | tf_op | source)
XLA Modules:
  0.0 86.4 jit_solution(12918631691229994755)
XLA Ops:
  0.6 83.8 %shard_map.86 = (f32[1,1536]{1,0:T(1,128)S(1)}, bf16[24,64,762]{2,1,0:T(8,128)(2,1)S(1)}) custom-call(bf16[24,64,762]{2,1,0:T(8,128)(2,1)} %background.1, s32[762]{0:T(1024)} %slab_owner.1, f32[16]{0:T(128)} %scale_table.1, s32[16]{0:T(128)} %reach_table.1, s32[6,1536]{1,0:T(8,128)} %x_class.1, s32[6,768]{1,0:T(8,128)} %y_class.1, s32[6,127]{1,0:T(8,128)} %z_class.1), custom_call_target="tpu_custom_call" | custom-call | tf_op jit(solution)/shard_map/pallas_call | solution.py:409
  84.4 0.6 copy.11
  85.0 1.4 %copy.12 = bf16[24,64,762]{2,1,0:T(8,128)(2,1)} copy(bf16[24,64,762]{2,1,0:T(8,128)(2,1)S(1)} %get-tuple-element.3) | data formatting | bytes 4681728

commit v4 on v3

--- a/solution.py
+++ b/solution.py
@@ -13,6 +13,7 @@
 PACK = 8
 HALF = 12
 STEP = 16
+TURN = 2
 F32 = jnp.float32
 BF16 = jnp.bfloat16
 
@@ -58,12 +59,12 @@
     size_y,
     lev,
     background,
-    slab_owner,
-    scale_table,
-    reach_table,
-    x_class,
-    y_class,
-    z_class,
+    slab_owner_hbm,
+    scale_table_hbm,
+    reach_table_hbm,
+    x_class_hbm,
+    y_class_hbm,
+    z_class_hbm,
     energy_out,
     cov_out,
     first_tile,
@@ -96,6 +97,14 @@
     sum_recv,
     row_send,
     row_recv,
+    greeted,
+    slab_owner,
+    scale_table,
+    reach_table,
+    x_class,
+    y_class,
+    z_class,
+    small_sem,
 ):
     lx, ly, nslab = background.shape
     nvar = z_class.shape[0]
@@ -116,15 +125,39 @@
     load_first.start()
     load = pltpu.make_async_copy(background, raw, raw_sem)
     load.start()
+    smalls = []
+    for k, (src, dst) in enumerate((
+        (slab_owner_hbm, slab_owner), (scale_table_hbm, scale_table), (reach_table_hbm, reach_table),
+        (x_class_hbm, x_class), (y_class_hbm, y_class), (z_class_hbm, z_class),
+    )):
+        smalls.append(pltpu.make_async_copy(src, dst, small_sem.at[k]))
+        smalls[-1].start()
     barrier = pltpu.get_barrier_semaphore()
 
-    @pl.loop(1, size_y, unroll=True)
-    def _(k):
-        pl.semaphore_signal(barrier, inc=1, device_id=at_y(k), device_id_type=MESH)
-
-    @pl.loop(1, size_x, unroll=unroll_x)
-    def _(k):
-        pl.semaphore_signal(barrier, inc=1, device_id=at_x(k), device_id_type=MESH)
+    near = (at_x(-2), at_x(-1), at_x(1), at_x(2), at_y(-1), at_y(1))
+    for peer in near:
+        pl.semaphore_signal(barrier, inc=1, device_id=peer, device_id_type=MESH)
+
+    def doublings(known, size):
+        reach = []
+        while known < size // 2:
+            reach.append(known)
+            known *= 2
+        return reach
+
+    rounds = max(len(doublings(2, size_x)), len(doublings(1, size_y)))
+
+    def greet(r):
+        for axis, at, reach in ((0, at_x, doublings(2, size_x)), (1, at_y, doublings(1, size_y))):
+            if r < len(reach):
+                for side, step in ((0, reach[r]), (1, -reach[r])):
+                    pl.semaphore_signal(greeted.at[axis, r, side], inc=1, device_id=at(step), device_id_type=MESH)
+
+    def heard(r):
+        for axis, reach in ((0, doublings(2, size_x)), (1, doublings(1, size_y))):
+            if r < len(reach):
+                for side in range(2):
+                    pl.semaphore_wait(greeted.at[axis, r, side], 1)
 
     outer = at_x(2 * core - 1)
     partner = at_x(1 - 2 * core)
@@ -135,29 +168,43 @@
             src_ref=src, dst_ref=dst, send_sem=send, recv_sem=recv, device_id=peer, device_id_type=MESH
         )
 
-    def to_outer(v):
-        own = win.at[v, :, pl.ds(REACH, lx)]
-        return remote(own, win.at[v, :, pl.ds(REACH + lx - 2 * lx * core, lx)], near_send.at[v, 0], near_recv.at[v, 0], outer)
-
-    def to_partner(v):
-        own = win.at[v, :, pl.ds(REACH, lx)]
-        return remote(own, win.at[v, :, pl.ds(far + 2 * lx * core, lx)], near_send.at[v, 1], near_recv.at[v, 1], partner)
-
-    def to_beyond(v):
-        own = win.at[v, :, pl.ds(REACH + (lx - far) * (1 - core), far)]
-        return remote(own, win.at[v, :, pl.ds((span - far) * core, far)], near_send.at[v, 2], near_recv.at[v, 2], beyond)
-
-    def forward(v):
-        got = win.at[v, :, pl.ds(far + (lx - far) + REACH * core, far)]
-        return remote(got, win.at[v, :, pl.ds((span - far) * core, far)], near_send.at[v, 3], near_recv.at[v, 3], partner)
-
-    def to_left(v):
-        own = xfw.at[v, :, pl.ds(REACH, REACH)]
-        return remote(own, xfw.at[v, :, pl.ds(REACH + ly, REACH)], side_send.at[v, 0], side_recv.at[v, 0], at_y(-1))
-
-    def to_right(v):
-        own = xfw.at[v, :, pl.ds(ly, REACH)]
-        return remote(own, xfw.at[v, :, pl.ds(0, REACH)], side_send.at[v, 1], side_recv.at[v, 1], at_y(1))
+    blocks = ly // PACK
+    cut = blocks // 2
+    units = [(v, 0, blocks) for v in range(nvar - 1)] + [(nvar - 1, 0, cut), (nvar - 1, cut, blocks - cut)]
+
+    def window(u, first, count):
+        return win.at[units[u][0], pl.ds(units[u][1], units[u][2]), pl.ds(first, count)]
+
+    def to_outer(u):
+        own = window(u, REACH, lx)
+        return remote(own, window(u, REACH + lx - 2 * lx * core, lx), near_send.at[u, 0], near_recv.at[u, 0], outer)
+
+    def to_partner(u):
+        own = window(u, REACH, lx)
+        return remote(own, window(u, far + 2 * lx * core, lx), near_send.at[u, 1], near_recv.at[u, 1], partner)
+
+    def to_beyond(u):
+        own = window(u, REACH + (lx - far) * (1 - core), far)
+        return remote(own, window(u, (span - far) * core, far), near_send.at[u, 2], near_recv.at[u, 2], beyond)
+
+    def forward(u):
+        got = window(u, far + (lx - far) + REACH * core, far)
+        return remote(got, window(u, (span - far) * core, far), near_send.at[u, 3], near_recv.at[u, 3], partner)
+
+    def columns(u):
+        if units[u][2] == blocks:
+            return 0, 0, REACH
+        return (TURN * PACK, 0, TURN * PACK) if units[u][1] == 0 else (0, TURN * PACK, TURN * PACK)
+
+    def to_left(u):
+        v, (first, _, count) = units[u][0], columns(u)
+        own = xfw.at[v, :, pl.ds(REACH + first, count)]
+        return remote(own, xfw.at[v, :, pl.ds(REACH + ly + first, count)], side_send.at[u, 0], side_recv.at[u, 0], at_y(-1))
+
+    def to_right(u):
+        v, (_, first, count) = units[u][0], columns(u)
+        own = xfw.at[v, :, pl.ds(ly + first, count)]
+        return remote(own, xfw.at[v, :, pl.ds(first, count)], side_send.at[u, 1], side_recv.at[u, 1], at_y(1))
 
     def align(v):
         rows = 4
@@ -169,28 +216,34 @@
                 i = block * rows + r
                 if LANES * (v + 1) > nslab:
                     win[v, :, REACH + i] = jnp.zeros((ly // PACK, PACK, LANES), BF16)
-                    piece = raw[i, :, lev * v : lev * (v + 1)]
-                    win[v, :, REACH + i, :, 0:lev] = piece.reshape(ly // PACK, PACK, lev)
+                    piece = raw[i, :, lev * v : lev * (v + 1)].reshape(blocks, PACK, lev)
+                    win[v, 0 : blocks - TURN, REACH + i, :, 0:lev] = piece[TURN:]
+                    win[v, blocks - TURN : blocks, REACH + i, :, 0:lev] = piece[:TURN]
                     continue
                 tile = (first_tile[i] if v == 0 else raw[i, :, LANES * v : LANES * (v + 1)]).astype(F32)
                 if v > 0:
                     before = raw[i, :, LANES * (v - 1) : LANES * v].astype(F32)
                     tile = pltpu.roll(jnp.where(column >= LANES - v, before, tile), v, 1)
                 tile = jnp.where(column < lev, tile, 0.0).astype(BF16)
-                win[v, :, REACH + i] = tile.reshape(ly // PACK, PACK, LANES)
+                tile = tile.reshape(blocks, PACK, LANES)
+                win[v, 0 : blocks - TURN, REACH + i] = tile[TURN:]
+                win[v, blocks - TURN : blocks, REACH + i] = tile[:TURN]
 
     load_first.wait()
     align(0)
-    pl.semaphore_wait(barrier, size_x + size_y - 2)
-    for v in range(nvar):
-        to_outer(v).start()
-        to_beyond(v).start()
-        to_partner(v).start()
-        if v == 0:
+    pl.semaphore_wait(barrier, len(near))
+    for u in range(len(units)):
+        to_outer(u).start()
+        to_beyond(u).start()
+        to_partner(u).start()
+        if u == 0:
+            greet(0)
             load.wait()
             align(1)
-        if v + 2 < nvar:
-            align(v + 2)
+        if u + 2 < nvar:
+            align(u + 2)
+    for copy in smalls:
+        copy.wait()
 
     n_x = size_x * lx
     n_y = size_y * ly
@@ -268,16 +321,25 @@
     rows_out[...] = jnp.zeros(rows_out.shape, F32)
     eye_x = (iota((size_x, LANES), 0) == iota((size_x, LANES), 1)).astype(BF16)
 
-    def filter_x(v):
+    def filter_x(u):
+        v, first_block, count = units[u]
         wide = 4
 
-        @pl.loop(0, ly // (wide * PACK))
-        def _(part):
-            blocks = [win[v, wide * part + k].reshape(span * PACK, LANES) for k in range(wide)]
-            got = dot_nn(kron[v], jnp.concatenate(blocks, 1)).reshape(lx, PACK, wide * LANES)
+        def some(at):
+            parts = [win[v, at + k].reshape(span * PACK, LANES) for k in range(wide)]
+            got = dot_nn(kron[v], jnp.concatenate(parts, 1)).reshape(lx, PACK, wide * LANES)
             for k in range(wide):
-                first = pl.multiple_of((wide * part + k) * PACK + REACH, PACK)
+                first = lax.rem(at + k + TURN, blocks) * PACK + REACH
+                first = first if isinstance(first, int) else pl.multiple_of(first, PACK)
                 xfw[v, :, pl.ds(first, PACK), :] = got[:, :, LANES * k : LANES * (k + 1)].astype(BF16)
+
+        if count == wide:
+            some(jnp.int32(first_block))
+        else:
+
+            @pl.loop(0, count // wide)
+            def _(step):
+                some(wide * step)
 
     def filter_y(v):
         rows = HALF
@@ -326,33 +388,46 @@
         to = lax.rem(p + k, size_x)
         return remote(rows_out.at[to], rows_in.at[p], row_send.at[k], row_recv.at[k], (to, q))
 
-    for v in range(nvar):
-        to_outer(v).wait_recv()
-        forward(v).start()
-        to_beyond(v).wait_recv()
-        to_partner(v).wait_recv()
-        forward(v).wait_recv()
-        filter_x(v)
-        to_left(v).start()
-        to_right(v).start()
-        if v >= 1:
-            to_left(v - 1).wait_recv()
-            to_right(v - 1).wait_recv()
-            filter_y(v - 1)
-            gather_slots(v - 1)
-        if v >= 2:
-            filter_z(v - 2)
+    def arrive(u):
+        to_outer(u).wait_recv()
+        forward(u).start()
+        to_beyond(u).wait_recv()
+        to_partner(u).wait_recv()
+        forward(u).wait_recv()
+        filter_x(u)
+        to_left(u).start()
+        to_right(u).start()
+
+    def sides(v):
+        for u in range(len(units)):
+            if units[u][0] == v:
+                to_left(u).wait_recv()
+                to_right(u).wait_recv()
+
+    heard(0)
+    greet(1)
+    for u in range(nvar):
+        arrive(u)
+        if u + 1 < rounds:
+            heard(u + 1)
+            greet(u + 2)
+        if u >= 1:
+            sides(u - 1)
+            filter_y(u - 1)
+            gather_slots(u - 1)
+        if 2 <= u < nvar - 1:
+            filter_z(u - 2)
     v = nvar - 1
-    to_left(v).wait_recv()
-    to_right(v).wait_recv()
+    arrive(nvar)
+    filter_z(v - 2)
+    sides(v)
     filter_y(v)
     gather_slots(v)
     for to in range(size_y):
         block = slots[:, LANES * to : LANES * (to + 1)]
         outbox[to] = block[0:STEP] + pltpu.roll(block[STEP : 2 * STEP], LANES // 2, 1)
 
-    @pl.loop(1, size_y, unroll=True)
-    def _(k):
+    for k in sorted(range(1, size_y), key=lambda k: abs(2 * k - size_y)):
         tell(k).start()
 
     filter_z(v - 1)
@@ -371,9 +446,13 @@
         picked = picked + dot_nt(eye_x, piece)
     rows_out[:, :, 0 : 2 * STEP] = picked.reshape(size_x, 1, 2 * STEP)
 
-    @pl.loop(1, size_x, unroll=unroll_x)
+    middle = size_x // 2
+    hand(middle).start()
+
+    @pl.loop(1, middle, unroll=3)
     def _(k):
-        hand(k).start()
+        hand(middle + k).start()
+        hand(middle - k).start()
 
     rows_in[p] = rows_out[p]
 
@@ -389,13 +468,13 @@
     wide_rows = wide_rows[0:size_x] + wide_rows[size_x : 2 * size_x] + wide_rows[2 * size_x :]
     energy_out[...] = jnp.sum(jnp.where(home, wide_rows, 0.0), 0, keepdims=True)
 
-    for v in range(nvar):
-        to_outer(v).wait_send()
-        to_beyond(v).wait_send()
-        to_partner(v).wait_send()
-        forward(v).wait_send()
-        to_left(v).wait_send()
-        to_right(v).wait_send()
+    for u in range(len(units)):
+        to_outer(u).wait_send()
+        to_beyond(u).wait_send()
+        to_partner(u).wait_send()
+        forward(u).wait_send()
+        to_left(u).wait_send()
+        to_right(u).wait_send()
 
 
 def per_device(background, slab_owner, class_length_scale, band_widths, x_class, y_class, z_class):
@@ -405,14 +484,13 @@
     size_y = lax.axis_size("sy")
     span = lx + 2 * REACH
     vmem = pl.BlockSpec(memory_space=pltpu.VMEM)
-    smem = pl.BlockSpec(memory_space=pltpu.SMEM)
     energy, cov = pl.pallas_call(
         functools.partial(kernel, size_x, size_y, lev),
         out_shape=(
             pltpu.VMEM((1, size_x * lx), F32),
             pltpu.VMEM((lx, ly, nslab), BF16),
         ),
-        in_specs=[pl.BlockSpec(memory_space=pl.ANY), vmem, smem, smem, vmem, vmem, vmem],
+        in_specs=[pl.BlockSpec(memory_space=pl.ANY)] * 7,
         out_specs=(vmem, vmem),
         scratch_shapes=[
             pltpu.VMEM((lx, ly, LANES), BF16),
@@ -437,14 +515,22 @@
             pltpu.VMEM((8, LANES), jnp.int32),
             pltpu.SemaphoreType.DMA,
             pltpu.SemaphoreType.DMA,
-            pltpu.SemaphoreType.DMA((nvar, 4)),
-            pltpu.SemaphoreType.DMA((nvar, 4)),
-            pltpu.SemaphoreType.DMA((nvar, 2)),
-            pltpu.SemaphoreType.DMA((nvar, 2)),
+            pltpu.SemaphoreType.DMA((nvar + 1, 4)),
+            pltpu.SemaphoreType.DMA((nvar + 1, 4)),
+            pltpu.SemaphoreType.DMA((nvar + 1, 2)),
+            pltpu.SemaphoreType.DMA((nvar + 1, 2)),
             pltpu.SemaphoreType.DMA((size_y,)),
             pltpu.SemaphoreType.DMA((size_y,)),
             pltpu.SemaphoreType.DMA((size_x,)),
             pltpu.SemaphoreType.DMA((size_x,)),
+            pltpu.SemaphoreType.REGULAR((2, 8, 2)),
+            pltpu.VMEM(slab_owner.shape, jnp.int32),
+            pltpu.SMEM(class_length_scale.shape, F32),
+            pltpu.SMEM(band_widths.shape, jnp.int32),
+            pltpu.VMEM(x_class.shape, jnp.int32),
+            pltpu.VMEM(y_class.shape, jnp.int32),
+            pltpu.VMEM(z_class.shape, jnp.int32),
+            pltpu.SemaphoreType.DMA((6,)),
         ],
         compiler_params=pltpu.CompilerParams(
             collective_id=0, has_side_effects=True, vmem_limit_bytes=60000 * 1024

time: 86.6 us -> 83.8 us (0.968)
  Pallas kernels: 83.8 us -> 81 us
    pallas_call x1, Pallas kernels: 83.8 us -> 81 us  [per_device(): pl.pallas_call(functools.partial(kernel, size_x, size_y, lev), out_shape=...]
where the time goes in v4:
time: 83.8 us; the launch traced here: 83.6 us
  Pallas kernels  81 us (97%)
  local copies, waits for them, and re-layouts  2 us (2%)
    pallas_call x1, Pallas kernels, per_device(): pl.pallas_call(functools.partial(kernel, size_x, size_y, lev), out_shape=...  81 us
    unnamed x2, local copies, waits for them, and re-layouts  2 us

profile of v4, /device:TPU:1, one launch (start us, length us, event | category | flops | bytes accessed | tf_op | source)
XLA Modules:
  0.0 83.6 jit_solution(11874954572793749661)
XLA Ops:
  0.6 81.0 %shard_map.86 = (f32[1,1536]{1,0:T(1,128)S(1)}, bf16[24,64,762]{2,1,0:T(8,128)(2,1)S(1)}) custom-call(bf16[24,64,762]{2,1,0:T(8,128)(2,1)} %background.1, s32[762]{0:T(1024)} %slab_owner_hbm.1, f32[16]{0:T(128)} %scale_table_hbm.1, s32[16]{0:T(128)} %reach_table_hbm.1, s32[6,1536]{1,0:T(8,128)} %x_class_hbm.1, s32[6,768]{1,0:T(8,128)} %y_class_hbm.1, ...), custom_call_target="tpu_custom_call" | custom-call | tf_op jit(solution)/shard_map/pallas_call | solution.py:487
  81.6 0.6 copy.11
  82.2 1.4 %copy.12 = bf16[24,64,762]{2,1,0:T(8,128)(2,1)} copy(bf16[24,64,762]{2,1,0:T(8,128)(2,1)S(1)} %get-tuple-element.3) | data formatting | bytes 4681728

commit v5 on v4

--- a/solution.py
+++ b/solution.py
@@ -13,7 +13,7 @@
 PACK = 8
 HALF = 12
 STEP = 16
-TURN = 2
+MIDDLE = 4
 F32 = jnp.float32
 BF16 = jnp.bfloat16
 
@@ -169,15 +169,22 @@
         )
 
     blocks = ly // PACK
-    cut = blocks // 2
-    units = [(v, 0, blocks) for v in range(nvar - 1)] + [(nvar - 1, 0, cut), (nvar - 1, cut, blocks - cut)]
+    order = list(range((blocks - MIDDLE) // 2, (blocks + MIDDLE) // 2))
+    for k in range((blocks - MIDDLE) // 2 - 1, -1, -1):
+        order += [k, blocks - 1 - k]
+    units = [(v, 0, blocks) for v in range(nvar - 1)]
+    units += [(nvar - 1, 0, MIDDLE)] + [(nvar - 1, k, 2) for k in range(MIDDLE, blocks, 2)]
 
     def window(u, first, count):
         return win.at[units[u][0], pl.ds(units[u][1], units[u][2]), pl.ds(first, count)]
 
+    def to_outer_edge(u):
+        own = window(u, REACH + (lx - far) * core, far)
+        return remote(own, window(u, REACH + lx - (lx + far) * core, far), near_send.at[u, 0], near_recv.at[u, 0], outer)
+
     def to_outer(u):
-        own = window(u, REACH, lx)
-        return remote(own, window(u, REACH + lx - 2 * lx * core, lx), near_send.at[u, 0], near_recv.at[u, 0], outer)
+        own = window(u, REACH + far - far * core, lx - far)
+        return remote(own, window(u, REACH + lx + far - (2 * lx + far) * core, lx - far), near_send.at[u, 4], near_recv.at[u, 4], outer)
 
     def to_partner(u):
         own = window(u, REACH, lx)
@@ -192,9 +199,11 @@
         return remote(got, window(u, (span - far) * core, far), near_send.at[u, 3], near_recv.at[u, 3], partner)
 
     def columns(u):
-        if units[u][2] == blocks:
-            return 0, 0, REACH
-        return (TURN * PACK, 0, TURN * PACK) if units[u][1] == 0 else (0, TURN * PACK, TURN * PACK)
+        _, first, count = units[u]
+        stored = order[first : first + count]
+        left = [k for k in stored if k < blocks // 2]
+        right = [k - blocks // 2 for k in stored if k >= blocks // 2]
+        return min(left) * PACK, min(right) * PACK, len(left) * PACK
 
     def to_left(u):
         v, (first, _, count) = units[u][0], columns(u)
@@ -217,8 +226,8 @@
                 if LANES * (v + 1) > nslab:
                     win[v, :, REACH + i] = jnp.zeros((ly // PACK, PACK, LANES), BF16)
                     piece = raw[i, :, lev * v : lev * (v + 1)].reshape(blocks, PACK, lev)
-                    win[v, 0 : blocks - TURN, REACH + i, :, 0:lev] = piece[TURN:]
-                    win[v, blocks - TURN : blocks, REACH + i, :, 0:lev] = piece[:TURN]
+                    for k in range(blocks):
+                        win[v, k, REACH + i, :, 0:lev] = piece[order[k]]
                     continue
                 tile = (first_tile[i] if v == 0 else raw[i, :, LANES * v : LANES * (v + 1)]).astype(F32)
                 if v > 0:
@@ -226,15 +235,16 @@
                     tile = pltpu.roll(jnp.where(column >= LANES - v, before, tile), v, 1)
                 tile = jnp.where(column < lev, tile, 0.0).astype(BF16)
                 tile = tile.reshape(blocks, PACK, LANES)
-                win[v, 0 : blocks - TURN, REACH + i] = tile[TURN:]
-                win[v, blocks - TURN : blocks, REACH + i] = tile[:TURN]
+                for k in range(blocks):
+                    win[v, k, REACH + i] = tile[order[k]]
 
     load_first.wait()
     align(0)
     pl.semaphore_wait(barrier, len(near))
     for u in range(len(units)):
+        to_outer_edge(u).start()
+        to_beyond(u).start()
         to_outer(u).start()
-        to_beyond(u).start()
         to_partner(u).start()
         if u == 0:
             greet(0)
@@ -323,23 +333,13 @@
 
     def filter_x(u):
         v, first_block, count = units[u]
-        wide = 4
-
-        def some(at):
+        wide = min(MIDDLE, count)
+        for at in range(first_block, first_block + count, wide):
             parts = [win[v, at + k].reshape(span * PACK, LANES) for k in range(wide)]
             got = dot_nn(kron[v], jnp.concatenate(parts, 1)).reshape(lx, PACK, wide * LANES)
             for k in range(wide):
-                first = lax.rem(at + k + TURN, blocks) * PACK + REACH
-                first = first if isinstance(first, int) else pl.multiple_of(first, PACK)
-                xfw[v, :, pl.ds(first, PACK), :] = got[:, :, LANES * k : LANES * (k + 1)].astype(BF16)
-
-        if count == wide:
-            some(jnp.int32(first_block))
-        else:
-
-            @pl.loop(0, count // wide)
-            def _(step):
-                some(wide * step)
+                first = order[at + k] * PACK + REACH
+                xfw[v, :, first : first + PACK, :] = got[:, :, LANES * k : LANES * (k + 1)].astype(BF16)
 
     def filter_y(v):
         rows = HALF
@@ -389,11 +389,12 @@
         return remote(rows_out.at[to], rows_in.at[p], row_send.at[k], row_recv.at[k], (to, q))
 
     def arrive(u):
-        to_outer(u).wait_recv()
+        to_outer_edge(u).wait_recv()
         forward(u).start()
         to_beyond(u).wait_recv()
         to_partner(u).wait_recv()
         forward(u).wait_recv()
+        to_outer(u).wait_recv()
         filter_x(u)
         to_left(u).start()
         to_right(u).start()
@@ -418,7 +419,8 @@
         if 2 <= u < nvar - 1:
             filter_z(u - 2)
     v = nvar - 1
-    arrive(nvar)
+    for u in range(nvar, len(units)):
+        arrive(u)
     filter_z(v - 2)
     sides(v)
     filter_y(v)
@@ -461,14 +463,21 @@
         hand(k).wait()
 
     arrived = rows_in[:, :, 0 : 2 * STEP].reshape(size_x, 2 * STEP)
-    column = iota((size_x, n_out), 1)
-    start = lx * iota((size_x, n_out), 0)
-    home = (column >= start) & (column < start + lx)
-    wide_rows = dot_nn(jnp.concatenate(split3(arrived), 0), table[...])
-    wide_rows = wide_rows[0:size_x] + wide_rows[size_x : 2 * size_x] + wide_rows[2 * size_x :]
-    energy_out[...] = jnp.sum(jnp.where(home, wide_rows, 0.0), 0, keepdims=True)
+    pieces = split3(arrived)
+    for low in range(0, n_out, LANES):
+        high = min(n_out, low + LANES)
+        top = low // lx // 8 * 8
+        end = min(size_x, -(-high // lx) + 7 - (-(-high // lx) + 7) % 8)
+        column = iota((end - top, high - low), 1) + low
+        start = lx * (iota((end - top, high - low), 0) + top)
+        home = (column >= start) & (column < start + lx)
+        got = jnp.zeros(home.shape, F32)
+        for piece in pieces:
+            got = got + dot_nn(piece[top:end], table[:, low:high])
+        energy_out[:, low:high] = jnp.sum(jnp.where(home, got, 0.0), 0, keepdims=True)
 
     for u in range(len(units)):
+        to_outer_edge(u).wait_send()
         to_outer(u).wait_send()
         to_beyond(u).wait_send()
         to_partner(u).wait_send()
@@ -515,10 +524,10 @@
             pltpu.VMEM((8, LANES), jnp.int32),
             pltpu.SemaphoreType.DMA,
             pltpu.SemaphoreType.DMA,
-            pltpu.SemaphoreType.DMA((nvar + 1, 4)),
-            pltpu.SemaphoreType.DMA((nvar + 1, 4)),
-            pltpu.SemaphoreType.DMA((nvar + 1, 2)),
-            pltpu.SemaphoreType.DMA((nvar + 1, 2)),
+            pltpu.SemaphoreType.DMA((nvar + 2, 5)),
+            pltpu.SemaphoreType.DMA((nvar + 2, 5)),
+            pltpu.SemaphoreType.DMA((nvar + 2, 2)),
+            pltpu.SemaphoreType.DMA((nvar + 2, 2)),
             pltpu.SemaphoreType.DMA((size_y,)),
             pltpu.SemaphoreType.DMA((size_y,)),
             pltpu.SemaphoreType.DMA((size_x,)),

time: 83.8 us -> 82.6 us (0.986)
  Pallas kernels: 81 us -> 79.8 us
    pallas_call x1, Pallas kernels: 81 us -> 79.8 us  [per_device(): pl.pallas_call(functools.partial(kernel, size_x, size_y, lev), out_shape=...]
where the time goes in v5:
time: 82.6 us; the launch traced here: 82.4 us
  Pallas kernels  79.8 us (97%)
  local copies, waits for them, and re-layouts  2 us (2%)
    pallas_call x1, Pallas kernels, per_device(): pl.pallas_call(functools.partial(kernel, size_x, size_y, lev), out_shape=...  79.8 us
    unnamed x2, local copies, waits for them, and re-layouts  2 us

profile of v5, /device:TPU:1, one launch (start us, length us, event | category | flops | bytes accessed | tf_op | source)
XLA Modules:
  0.0 82.4 jit_solution(7477606972342688289)
XLA Ops:
  0.6 79.8 %shard_map.86 = (f32[1,1536]{1,0:T(1,128)S(1)}, bf16[24,64,762]{2,1,0:T(8,128)(2,1)S(1)}) custom-call(bf16[24,64,762]{2,1,0:T(8,128)(2,1)} %background.1, s32[762]{0:T(1024)} %slab_owner_hbm.1, f32[16]{0:T(128)} %scale_table_hbm.1, s32[16]{0:T(128)} %reach_table_hbm.1, s32[6,1536]{1,0:T(8,128)} %x_class_hbm.1, s32[6,768]{1,0:T(8,128)} %y_class_hbm.1, ...), custom_call_target="tpu_custom_call" | custom-call | tf_op jit(solution)/shard_map/pallas_call | solution.py:496
  80.4 0.6 copy.11
  81.0 1.4 %copy.12 = bf16[24,64,762]{2,1,0:T(8,128)(2,1)} copy(bf16[24,64,762]{2,1,0:T(8,128)(2,1)S(1)} %get-tuple-element.3) | data formatting | bytes 4681728

commit v6 on v5

--- a/solution.py
+++ b/solution.py
@@ -67,7 +67,6 @@
     z_class_hbm,
     energy_out,
     cov_out,
-    first_tile,
     raw,
     win,
     xfw,
@@ -121,8 +120,15 @@
     def at_y(step):
         return (p, lax.rem(q + step + size_y, size_y))
 
-    load_first = pltpu.make_async_copy(background.at[:, :, 0:LANES], first_tile, first_sem)
-    load_first.start()
+    blocks = ly // PACK
+    order = list(range((blocks - MIDDLE) // 2, (blocks + MIDDLE) // 2))
+    for k in range((blocks - MIDDLE) // 2 - 1, -1, -1):
+        order += [k, blocks - 1 - k]
+    firsts = []
+    for k in range(blocks):
+        rows = background.at[:, order[k] * PACK : (order[k] + 1) * PACK, 0:LANES]
+        firsts.append(pltpu.make_async_copy(rows, win.at[0, k, REACH : REACH + lx], first_sem.at[k]))
+        firsts[-1].start()
     load = pltpu.make_async_copy(background, raw, raw_sem)
     load.start()
     smalls = []
@@ -168,10 +174,6 @@
             src_ref=src, dst_ref=dst, send_sem=send, recv_sem=recv, device_id=peer, device_id_type=MESH
         )
 
-    blocks = ly // PACK
-    order = list(range((blocks - MIDDLE) // 2, (blocks + MIDDLE) // 2))
-    for k in range((blocks - MIDDLE) // 2 - 1, -1, -1):
-        order += [k, blocks - 1 - k]
     units = [(v, 0, blocks) for v in range(nvar - 1)]
     units += [(nvar - 1, 0, MIDDLE)] + [(nvar - 1, k, 2) for k in range(MIDDLE, blocks, 2)]
 
@@ -229,17 +231,16 @@
                     for k in range(blocks):
                         win[v, k, REACH + i, :, 0:lev] = piece[order[k]]
                     continue
-                tile = (first_tile[i] if v == 0 else raw[i, :, LANES * v : LANES * (v + 1)]).astype(F32)
-                if v > 0:
-                    before = raw[i, :, LANES * (v - 1) : LANES * v].astype(F32)
-                    tile = pltpu.roll(jnp.where(column >= LANES - v, before, tile), v, 1)
+                tile = raw[i, :, LANES * v : LANES * (v + 1)].astype(F32)
+                before = raw[i, :, LANES * (v - 1) : LANES * v].astype(F32)
+                tile = pltpu.roll(jnp.where(column >= LANES - v, before, tile), v, 1)
                 tile = jnp.where(column < lev, tile, 0.0).astype(BF16)
                 tile = tile.reshape(blocks, PACK, LANES)
                 for k in range(blocks):
                     win[v, k, REACH + i] = tile[order[k]]
 
-    load_first.wait()
-    align(0)
+    for copy in firsts:
+        copy.wait()
     pl.semaphore_wait(barrier, len(near))
     for u in range(len(units)):
         to_outer_edge(u).start()
@@ -427,7 +428,7 @@
     gather_slots(v)
     for to in range(size_y):
         block = slots[:, LANES * to : LANES * (to + 1)]
-        outbox[to] = block[0:STEP] + pltpu.roll(block[STEP : 2 * STEP], LANES // 2, 1)
+        outbox[to] = (block[0:STEP] + pltpu.roll(block[STEP : 2 * STEP], LANES // 2, 1)).astype(BF16)
 
     for k in sorted(range(1, size_y), key=lambda k: abs(2 * k - size_y)):
         tell(k).start()
@@ -439,9 +440,9 @@
     def _(k):
         tell(k).wait()
 
-    total = outbox[q]
+    total = outbox[q].astype(F32)
     for k in range(1, size_y):
-        total = total + inbox[k]
+        total = total + inbox[k].astype(F32)
     both = jnp.concatenate([total, pltpu.roll(total, LANES // 2, 1)], 0)
     picked = jnp.zeros((size_x, 2 * STEP), F32)
     for piece in split3(both):
@@ -502,7 +503,6 @@
         in_specs=[pl.BlockSpec(memory_space=pl.ANY)] * 7,
         out_specs=(vmem, vmem),
         scratch_shapes=[
-            pltpu.VMEM((lx, ly, LANES), BF16),
             pltpu.VMEM((lx, ly, nslab), BF16),
             pltpu.VMEM((nvar, ly // PACK, span, PACK, LANES), BF16),
             pltpu.VMEM((nvar, lx, ly + 2 * REACH, LANES), BF16),
@@ -516,13 +516,13 @@
             pltpu.VMEM((nvar, size_y * LANES, LANES), BF16),
             pltpu.VMEM((nvar, 2 * STEP, LANES), F32),
             pltpu.VMEM((2 * STEP, size_y * LANES), F32),
-            pltpu.VMEM((size_y, STEP, LANES), F32),
-            pltpu.VMEM((size_y, STEP, LANES), F32),
+            pltpu.VMEM((size_y, STEP, LANES), BF16),
+            pltpu.VMEM((size_y, STEP, LANES), BF16),
             pltpu.VMEM((size_x, 1, LANES), F32),
             pltpu.VMEM((size_x, 1, LANES), F32),
             pltpu.VMEM((2 * STEP, size_x * lx), BF16),
             pltpu.VMEM((8, LANES), jnp.int32),
-            pltpu.SemaphoreType.DMA,
+            pltpu.SemaphoreType.DMA((ly // PACK,)),
             pltpu.SemaphoreType.DMA,
             pltpu.SemaphoreType.DMA((nvar + 2, 5)),
             pltpu.SemaphoreType.DMA((nvar + 2, 5)),

time: 82.6 us -> 82.2 us (level)
  no operation moved by 1% of the time
where the time goes in v6:
time: 82.2 us; the launch traced here: 82.1 us
  Pallas kernels  79.4 us (97%)
  local copies, waits for them, and re-layouts  2 us (2%)
    pallas_call x1, Pallas kernels, per_device(): pl.pallas_call(functools.partial(kernel, size_x, size_y, lev), out_shape=...  79.4 us
    unnamed x2, local copies, waits for them, and re-layouts  2 us

profile of v6, /device:TPU:1, one launch (start us, length us, event | category | flops | bytes accessed | tf_op | source)
XLA Modules:
  0.0 82.1 jit_solution(16792821924385180310)
XLA Ops:
  0.6 79.4 %shard_map.86 = (f32[1,1536]{1,0:T(1,128)S(1)}, bf16[24,64,762]{2,1,0:T(8,128)(2,1)S(1)}) custom-call(bf16[24,64,762]{2,1,0:T(8,128)(2,1)} %background.1, s32[762]{0:T(1024)} %slab_owner_hbm.1, f32[16]{0:T(128)} %scale_table_hbm.1, s32[16]{0:T(128)} %reach_table_hbm.1, s32[6,1536]{1,0:T(8,128)} %x_class_hbm.1, s32[6,768]{1,0:T(8,128)} %y_class_hbm.1, ...), custom_call_target="tpu_custom_call" | custom-call | tf_op jit(solution)/shard_map/pallas_call | solution.py:497
  80.1 0.6 copy.11
  80.7 1.4 %copy.12 = bf16[24,64,762]{2,1,0:T(8,128)(2,1)} copy(bf16[24,64,762]{2,1,0:T(8,128)(2,1)S(1)} %get-tuple-element.3) | data formatting | bytes 4681728
